TPU v7x, 256 devices: a whole 4x4x8 slice. The times are simulated.
256 devices in a mesh: segment: 2 (over x_lo), seq: 16 (over y, x_hi, core), mp: 8 (over z).
Axes of the slice: x: 4 (x_hi: 2, x_lo: 2; x = x_hi * 2 + x_lo), y: 4, z: 8, core: 2. Of those that a mesh axis runs over, the one named last changes fastest.
Arguments:
- enc_states: bfloat16 [4096, 4096], P('seq', 'mp'), may hold values from -6 to 6
- dec_states: bfloat16 [4096, 4096], P('seq', 'mp'), may hold values from -21 to 21
- section_weights: bfloat16 [2, 4096, 2, 4096], P('segment', None, None, 'mp'), may hold values from -3 to 3
- group_lengths: int32 [32], P('seq'), may hold values from 1 to 128, 3072 in all
Outputs:
- mixed: bfloat16 [4096, 4096], P('seq', ('segment', 'mp'))
Inputs may be any that keep to these rules, and one draw needn't show every extreme that they name: Rows c * 128 to c * 128 + group_lengths[c] - 1 of the memory are real, the rest of block c is padding.
All inputs are finite; a program needn't handle non-finite values.
Results may differ from a plain program's by a relative error of at most 0.018.
Values may be sent and summed in bfloat16 or wider, within the bound.
A program may use at most 128 MiB of HBM per device.

v0:
```python
import math

import jax
import jax.numpy as jnp
from jax import lax
from jax.sharding import PartitionSpec as P

DH = 256
GROUP = 128


def from_behind(value, axis, steps):
    count = lax.axis_size(axis)
    leading, last = (max(0, -steps), min(count, count - steps))
    return lax.ppermute(value, axis, [(source, source + steps) for source in range(leading, last)])


def local(enc_states, dec_states, section_weights, group_lengths):
    encoder_side = lax.axis_index("segment") == 0
    local_weight = section_weights[0]
    width = local_weight.shape[0]
    columns = local_weight.shape[2]
    enc_rows = enc_states.shape[0]
    dec_rows = dec_states.shape[0]
    heads = columns // DH
    scale = DH ** (-0.5)
    start_sums = (
        jnp.zeros((enc_rows, 2 * columns), jnp.float32),
        jnp.zeros((dec_rows, columns), jnp.float32),
    )
    pieces = (
        lax.all_gather(enc_states, "mp", axis=1, tiled=True),
        lax.all_gather(dec_states, "mp", axis=1, tiled=True),
    )
    rows_in = pieces[0].shape[1]

    def encoder_work(state):
        update = jnp.dot(
            pieces[0],
            local_weight.reshape(rows_in, 2 * columns),
            preferred_element_type=jnp.float32,
        )
        return (update, state[1])

    def decoder_work(state):
        update = jnp.dot(pieces[1], local_weight[:, 0, :], preferred_element_type=jnp.float32)
        return (state[0], update)

    memory_sum, query_sum = lax.cond(encoder_side, encoder_work, decoder_work, start_sums)
    memory = memory_sum.astype(jnp.bfloat16)
    queries = query_sum.astype(jnp.bfloat16).reshape(dec_rows, heads, DH)
    received = from_behind(memory, "segment", 1)
    start_state = (
        jnp.full((dec_rows, heads), -1e30, jnp.float32),
        jnp.zeros((dec_rows, heads), jnp.float32),
        jnp.zeros((dec_rows, heads, DH), jnp.float32),
    )
    carry = start_state
    memory_piece = lax.all_gather(received, "seq", axis=0, tiled=True)
    length_piece = lax.all_gather(group_lengths, "seq", axis=0, tiled=True)
    amount = memory_piece.shape[0]
    span = math.gcd(amount, 1024)
    block_total = amount // span
    memory_blocks = memory_piece.reshape(block_total, span, 2 * columns)
    length_blocks = length_piece.reshape(block_total, span // GROUP)

    def one_block(state, item):
        best, total, accum = state
        block, lengths = item
        block_keys = block[:, :columns].reshape(span, heads, DH)
        block_values = block[:, columns:].reshape(span, heads, DH)
        scores = (
            jnp.einsum("qhd,khd->qhk", queries, block_keys, preferred_element_type=jnp.float32)
            * scale
        )
        valid = (jnp.arange(GROUP)[None, :] < lengths[:, None]).reshape(span)
        scores = jnp.where(valid[None, None, :], scores, -1e30)
        new_best = jnp.maximum(best, jnp.max(scores, axis=2))
        shrink = jnp.exp(best - new_best)
        weights = jnp.exp(scores - new_best[:, :, None]).astype(jnp.bfloat16)
        total = total * shrink + jnp.sum(weights, axis=2, dtype=jnp.float32)
        accum = accum * shrink[:, :, None] + jnp.einsum(
            "qhk,khd->qhd", weights, block_values, preferred_element_type=jnp.float32
        )
        return ((new_best, total, accum), None)

    carry, _ = lax.scan(one_block, carry, (memory_blocks, length_blocks))
    best, total, accum = carry
    attended = (accum / total[:, :, None]).astype(jnp.bfloat16).reshape(dec_rows, columns)

    def no_term(operand):
        return jnp.zeros((dec_rows, width), jnp.float32)

    def output_term(operand):
        projected = lax.dot_general(
            operand,
            local_weight[:, 1, :],
            (((1,), (1,)), ((), ())),
            preferred_element_type=jnp.float32,
        )
        offset = lax.axis_index("mp") * columns
        current = lax.dynamic_slice_in_dim(projected, offset, columns, 1)
        return lax.dynamic_update_slice_in_dim(
            projected, current + dec_states.astype(jnp.float32), offset, 1
        )

    term = lax.cond(encoder_side, no_term, output_term, attended)
    return lax.psum_scatter(
        term.astype(jnp.bfloat16), ("segment", "mp"), scatter_dimension=1, tiled=True
    )


def solution(mesh):
    in_specs = (P("seq", "mp"), P("seq", "mp"), P("segment", None, None, "mp"), P("seq"))
    out_specs = P("seq", ("segment", "mp"))
    return jax.shard_map(local, mesh=mesh, in_specs=in_specs, out_specs=out_specs, check_vma=False)
```

profile of v0, /device:TPU:2, one launch (start us, length us, event | category | flops | bytes accessed | tf_op | source)
XLA Modules:
  0.0 327.3 jit_solution(9274638926449847188)
XLA Ops:
  6.5 0.7 all-gather.6.cloned.1.call-update
  7.3 0.0 all-gather.4.cloned.1.call-start
  7.3 0.7 all-gather.4.cloned.1.call-update
  8.0 0.0 all-gather.8.cloned.1.call-start
  8.1 8.0 %copy.20 = bf16[1,4096,2,512]{3,1,2,0:T(8,128)(2,1)} copy(bf16[1,4096,2,512]{3,2,1,0:T(2,128)(2,1)} %param.12) | data formatting | bytes 16777216 | tf_op args[2]
  16.0 37.2 %all-gather.6.cloned.1.call-done = bf16[256,4096]{1,0:T(8,128)(2,1)} async-done(((bf16[256,512]{1,0:T(8,128)(2,1)}), bf16[256,4096]{1,0:T(8,128)(2,1)}) %all-gather.6.cloned.1.call-update) | async-done | bytes 2097168 | tf_op jit(solution)/shard_map/all_gather | solution.py:32
  53.2 41.5 %all-gather.4.cloned.1.call-done = bf16[256,4096]{1,0:T(8,128)(2,1)} async-done(((bf16[256,512]{1,0:T(8,128)(2,1)}), bf16[256,4096]{1,0:T(8,128)(2,1)}) %all-gather.4.cloned.1.call-update) | async-done | bytes 2097168 | tf_op jit(solution)/shard_map/all_gather | solution.py:33
  94.7 4.2 %conditional.2 = (bf16[256,1024]{1,0:T(8,128)(2,1)S(1)}, bf16[256,512]{1,0:T(8,128)(2,1)S(1)}) conditional(s32[]{:T(128)} %convert_element_type.25, (bf16[4096,2,512]{2,0,1:T(8,128)(2,1)}, bf16[256,4096]{1,0:T(8,128)(2,1)}) %tuple.67, (bf16[1,4096,2,512]{3,2,1,0:T(2,128)(2,1)}, bf16[256,4096]{1,0:T(8,128)(2,1)}) %tuple.24), branch_computations={%region_0.0_spmd, %region_1.0_spmd} | conditional | flops 2147483648 | bytes 36438064 | solution.py:49
  94.7 4.1 %fusion = bf16[256,512]{1,0:T(8,128)(2,1)S(1)} fusion(bf16[256,4096]{1,0:T(8,128)(2,1)} %get-tuple-element.51, bf16[4096,2,512]{2,0,1:T(8,128)(2,1)} %get-tuple-element.52), kind=kOutput, calls=%fused_computation | convolution fusion | flops 1073741824 | bytes 6553600 | tf_op jit(solution)/shard_map/cond/branch_0_fun/dot_general | solution.py:46
  98.8 0.1 broadcast_in_dim.17
  98.9 1.3 collective-permute-start
  100.2 19.8 %collective-permute-done = bf16[256,1024]{1,0:T(8,128)(2,1)S(1)} collective-permute-done((bf16[256,1024]{1,0:T(8,128)(2,1)S(1)}, bf16[256,1024]{1,0:T(8,128)(2,1)S(1)}, u32[]{:S(2)}, u32[]{:S(2)}) %collective-permute-start) | collective-permute-done | bytes 524320 | tf_op jit(solution)/shard_map/ppermute | solution.py:15
  120.0 0.8 copy-done.3
  120.9 0.0 reduce-scatter.2.cloned.1.call-start
  121.0 0.6 dynamic-slice
  122.3 0.2 dynamic-update-slice
  122.5 13.2 %all-reduce = s32[32]{0:T(128)S(1)} all-reduce(s32[32]{0:T(128)S(1)} %dynamic-update-slice), channel_id=1, replica_groups=mesh['segment'=2,'seq'=16,'mp'=8] {'seq'}, use_global_device_ids=true, to_apply=%add | all-reduce | flops 32 | bytes 256
  135.7 0.1 reshape.39
  135.8 0.1 copy.10
  135.9 0.1 copy.12
  136.1 60.6 %all-gather.8.cloned.1.call-done = bf16[4096,1024]{1,0:T(8,128)(2,1)} async-done(((bf16[256,1024]{1,0:T(8,128)(2,1)}), bf16[4096,1024]{1,0:T(8,128)(2,1)}) %all-gather.8.cloned.1.call-update) | async-done | bytes 8388624 | tf_op jit(solution)/shard_map/all_gather | solution.py:59
  196.7 39.4 %while.15 = (s32[]{:T(128)}, f32[256,2]{0,1:T(2,128)S(1)}, f32[256,2]{0,1:T(2,128)S(1)}, f32[256,2,256]{0,2,1:T(8,128)}, s32[4,8]{1,0:T(4,128)S(1)}, /*index=5*/...) while((s32[]{:T(128)}, f32[256,2]{0,1:T(2,128)S(1)}, ...), condition=%wide.region_5.6_spmd.clone, body=%wide.region_2.5_spmd.clone.sunk | while | flops 544083456 | bytes 26513672 | solution.py:87
  196.7 0.1 fusion.35
  196.8 3.1 constant_dynamic-slice_fusion.2
  199.9 2.9 copy.22
  202.8 0.2 fusion.36
  203.0 1.0 bitcast_reduce_fusion.2
  204.0 0.5 convert_reduce_fusion.2
  204.5 0.5 copy-done.1
  205.0 0.7 fusion.39
  205.8 0.8 copy-done.2
  206.6 0.1 fusion.35
  206.7 3.1 constant_dynamic-slice_fusion.2
  209.8 2.9 copy.22
  212.6 0.2 fusion.36
  212.8 1.0 bitcast_reduce_fusion.2
  213.8 0.5 convert_reduce_fusion.2
  214.4 0.5 copy-done.1
  214.9 0.7 fusion.39
  215.6 0.8 copy-done.2
  216.4 0.1 fusion.35
  216.5 3.1 constant_dynamic-slice_fusion.2
  219.6 2.9 copy.22
  222.5 0.2 fusion.36
  222.7 1.0 bitcast_reduce_fusion.2
  223.7 0.5 convert_reduce_fusion.2
  224.2 0.5 copy-done.1
  224.7 0.7 fusion.39
  225.5 0.8 copy-done.2
  226.3 0.1 fusion.35
  226.4 3.1 constant_dynamic-slice_fusion.2
  229.5 2.9 copy.22
  232.3 0.2 fusion.36
  232.5 1.0 bitcast_reduce_fusion.2
  233.6 0.5 convert_reduce_fusion.2
  234.1 0.5 copy-done.1
  234.6 0.7 fusion.39
  235.3 0.8 copy-done.2
  236.1 1.1 divide_convert_fusion
  237.2 7.5 %conditional.3 = (f32[256,4096]{1,0:T(8,128)}) conditional(s32[]{:T(128)} %convert_element_type.25, (bf16[256,2,256]{0,2,1:T(8,128)(2,1)S(1)}, bf16[4096,2,512]{2,0,1:T(8,128)(2,1)}, bf16[256,512]{1,0:T(8,128)(2,1)}) %tuple.68, () %tuple.27), branch_computations={%region_6.7_spmd, %region_7.8_spmd} | conditional | flops 1074003968 | bytes 11010154 | solution.py:107
  237.3 5.5 %fusion.3 = f32[256,4096]{1,0:T(8,128)} fusion(bf16[256,512]{0,1:T(8,128)(2,1)S(1)} %bitcast.76, bf16[4096,2,512]{2,0,1:T(8,128)(2,1)} %get-tuple-element.64), kind=kOutput, calls=%fused_computation.3 | convolution fusion | flops 1073741824 | bytes 8650752 | tf_op jit(solution)/shard_map/cond/branch_0_fun/dot_general | solution.py:95
  242.8 2.0 add_dynamic-update-slice_fusion
  244.7 3.8 %convert_element_type.29 = bf16[256,4096]{1,0:T(8,128)(2,1)} convert(f32[256,4096]{1,0:T(8,128)} %get-tuple-element.217) | non-fusion elementwise | flops 1048576 | bytes 6291456 | tf_op jit(solution)/shard_map/convert_element_type | solution.py:109
  248.6 72.2 %reduce-scatter.2.cloned.1.call-done = bf16[256,256]{1,0:T(8,128)(2,1)} async-done(((bf16[256,4096]{1,0:T(8,128)(2,1)}), bf16[256,256]{1,0:T(8,128)(2,1)}) %reduce-scatter.2.cloned.1.call-update) | async-done | bytes 131088 | tf_op jit(solution)/shard_map/reduce_scatter | solution.py:108
  (38 shorter events, 0.2 us)
Async XLA Ops:
  6.5 46.7 %all-gather.6.cloned.1.call-start = ((), (), s32[]{:S(2)}) async-start(), calls=%async_computation.2 | async-start | bytes 2359296 | tf_op jit(solution)/shard_map/all_gather | solution.py:32
  7.3 87.5 %all-gather.4.cloned.1.call-start = ((), (), s32[]{:S(2)}) async-start(), calls=%async_computation.1 | async-start | bytes 2359296 | tf_op jit(solution)/shard_map/all_gather | solution.py:33
  8.0 188.7 %all-gather.8.cloned.1.call-start = ((), (), s32[]{:S(2)}) async-start(), calls=%async_computation.3 | async-start | bytes 8912896 | tf_op jit(solution)/shard_map/all_gather | solution.py:59
  94.7 26.2 %copy-start.6 = (u32[256]{0:T(256)S(1)}, u32[256]{0:T(256)}, u32[]{:S(2)}) copy-start(u32[256]{0:T(256)} %constant.50) | copy-start | bytes 3076
  94.7 27.5 %copy-start.5 = (s32[2]{0:T(128)S(1)}, s32[2]{0:T(128)}, u32[]{:S(2)}) copy-start(s32[2]{0:T(128)} %param.13) | copy-start | bytes 28
  98.9 21.1 %collective-permute-start = (bf16[256,1024]{1,0:T(8,128)(2,1)S(1)}, bf16[256,1024]{1,0:T(8,128)(2,1)S(1)}, u32[]{:S(2)}, u32[]{:S(2)}) collective-permute-start(bf16[256,1024]{1,0:T(8,128)(2,1)S(1)} %get-tuple-element.70), channel_id=1, source_target_pairs={{0,128},{1,129},{2,130},{3,131},{4,132},{5,133},{6,134},{7,135},{8... | collective-permute-start | bytes 1572872 | tf_op jit(solution)/shard_map/ppermute | solution.py:15
  120.0 0.8 copy-start.3
  120.9 199.9 %reduce-scatter.2.cloned.1.call-start = ((), (), s32[]{:S(2)}) async-start(), calls=%async_computation.4 | async-start | bytes 2228224 | tf_op jit(solution)/shard_map/reduce_scatter | solution.py:108
  204.0 1.0 copy-start.1
  205.8 0.8 copy-start.2
  213.8 1.0 copy-start.1
  215.6 0.8 copy-start.2
  223.7 1.0 copy-start.1
  225.5 0.8 copy-start.2
  233.5 1.0 copy-start.1
  235.3 0.8 copy-start.2
  237.2 5.5 %copy-start = (bf16[256,512]{1,0:T(8,128)(2,1)S(1)}, bf16[256,512]{1,0:T(8,128)(2,1)}, u32[]{:S(2)}) copy-start(bf16[256,512]{1,0:T(8,128)(2,1)} %get-tuple-element.65) | copy-start | bytes 786436 | tf_op jit(solution)/shard_map/cond
Sparse Core Ops, SparseCore 0:
  9.1 44.0 all-gather.5
  55.0 39.6 all-gather.3
  121.0 75.6 all-gather.7
  248.7 72.0 reduce-scatter.1
where the time goes:
time: 329 us; the launch traced here: 327 us
  waiting for transfers between devices  233 us (71%)
  local copies, waits for them, and re-layouts  39.8 us (12%)
  matrix products  16.6 us (5%)
  between operations  13.9 us (4%)
  blocking collectives  13.2 us (4%)
  other arithmetic  9.28 us (3%)
    reduce_scatter x1, waiting for transfers between devices, local(): lax.psum_scatter(term.astype(jnp.bfloat16), ('segment', 'mp'), scatter_di...  72.2 us
    all_gather x1, waiting for transfers between devices, local(): memory_piece = lax.all_gather(received, 'seq', axis=0, tiled=True)  60.6 us
    all_gather x1, waiting for transfers between devices, local(): lax.all_gather(dec_states, 'mp', axis=1, tiled=True)  41.5 us
    all_gather x1, waiting for transfers between devices, local(): lax.all_gather(enc_states, 'mp', axis=1, tiled=True)  37.2 us
    dynamic_slice x8, local copies, waits for them, and re-layouts, local(): carry, _ = lax.scan(one_block, carry, (memory_blocks, length_blocks))  23.8 us
    ppermute x1, waiting for transfers between devices, from_behind(): lax.ppermute(value, axis, [(source, source + steps) for source in range(l...  19.8 us
    unnamed x1, blocking collectives  13.2 us
    unnamed x11, local copies, waits for them, and re-layouts  9.78 us
  transfers between devices with their start and end apart: 5, of which 5 were waited for; matrix products, arithmetic and copies ran while one was open for 3% of the time, Pallas kernels for 0%

commit v1 on v0

v1 whole, which is shorter than its diff:
```python
import jax
import jax.numpy as jnp
from jax import lax
from jax.experimental import pallas as pl
from jax.experimental.pallas import tpu as pltpu
from jax.sharding import PartitionSpec as P

MESH = pl.DeviceIdType.MESH
F32, BF16 = jnp.float32, jnp.bfloat16
DH, GROUP = 256, 128
ROWS, FEAT, NZ, NSEQ = 256, 512, 8, 16
HALF, QUART = ROWS // 2, ROWS // 4
BLOCK = 2 * GROUP + 16
NEG = -1e30
DEINT = 32
OFFSETS = (0, -1, 1, -2, 2, -3, 3, 4)
REACH = {("R", 0): 4, ("R", 1): 3, ("L", 1): 4, ("L", 0): 3}
STREAMS = (("R", 0), ("L", 1), ("R", 1), ("L", 0))
NT = (((1,), (1,)), ((), ()))


def slot_of(direction, distance):
    if distance == 0:
        return 0
    if distance == 4:
        return 7
    return 2 * distance - (1 if direction == "R" else 0)


def kernel(enc, dec, weights, lengths, out, xg, stage, w0, w1, wo, acc, kv, kvs, qbuf, qs, dres, att, oacc,
           mx, den, pacc, sbuf, rbuf, load_sem, stage_sem, z_send, z_recv, kv_send, kv_recv, q_send, q_recv,
           wo_send, wo_recv, at_send, at_recv, rs_send, rs_recv):
    s = lax.axis_index("segment")
    q = lax.axis_index("seq")
    m = lax.axis_index("mp")
    y, xh, c = q // 4, (q // 2) % 2, q % 2
    z_to = {"R": (m + 1) % NZ, "L": (m + NZ - 1) % NZ}

    def seq_of(yy, hh, cc):
        return (yy * 2 + hh) * 2 + cc

    y_up, y_down, y_far = (y + 1) % 4, (y + 3) % 4, (y + 2) % 4
    partner = (s, seq_of(y, xh, 1 - c), m)
    up, down = (s, seq_of(y_up, xh, c), m), (s, seq_of(y_down, xh, c), m)
    across = (1 - s, q, m)
    across_other = (1 - s, seq_of(y, 1 - xh, c), m)
    same_other = (s, seq_of(y, 1 - xh, c), m)
    z_dev = {d: (s, q, z_to[d]) for d in ("R", "L")}

    def remote(src, dst, send, recv, device):
        return pltpu.make_async_remote_copy(
            src_ref=src, dst_ref=dst, send_sem=send, recv_sem=recv, device_id=device, device_id_type=MESH
        )

    def load_x(source):
        return pltpu.make_async_copy(source, xg.at[0], load_sem.at[0])

    @pl.when(s == 0)
    def _():
        load_x(enc).start()

    @pl.when(s == 1)
    def _():
        load_x(dec).start()

    load_res = pltpu.make_async_copy(dec, dres, load_sem.at[1])
    load_res.start()

    def shard_of(o):
        return (m + NZ + OFFSETS[o]) % NZ

    def stage_copy(o):
        rows = pl.ds(pl.multiple_of(shard_of(o) * FEAT, FEAT), FEAT)
        return pltpu.make_async_copy(weights.at[0, rows], stage.at[o % 2], stage_sem.at[o % 2])

    stage_copy(0).start()
    stage_copy(1).start()

    barrier = pltpu.get_barrier_semaphore()
    peers = (z_dev["R"], z_dev["L"], up, down, partner, across, across_other, same_other)
    for peer in peers:
        pl.semaphore_signal(barrier, inc=1, device_id=peer, device_id_type=MESH)
    pl.semaphore_wait(barrier, len(peers))

    def z_copy(half, stream, distance):
        direction, sub = stream
        rows = pl.ds(half * HALF + sub * QUART, QUART)
        k = STREAMS.index(stream)
        sems = (half * 4 + k) * 4 + distance - 1
        return remote(
            xg.at[slot_of(direction, distance - 1), rows],
            xg.at[slot_of(direction, distance), rows],
            z_send.at[sems],
            z_recv.at[sems],
            z_dev[direction],
        )

    def z_start(half):
        for stream in STREAMS:
            z_copy(half, stream, 1).start()

    def z_step(half, distance):
        for stream in STREAMS:
            if distance <= REACH[stream]:
                z_copy(half, stream, distance).wait_recv()
                if distance < REACH[stream]:
                    z_copy(half, stream, distance + 1).start()

    def split(o):
        stage_copy(o).wait()
        j = shard_of(o)

        def body(i, carry):
            r = pl.multiple_of(i * DEINT, DEINT)
            pair = jnp.swapaxes(stage[o % 2, pl.ds(r, DEINT)], 0, 1)
            w0[o, pl.ds(r, DEINT), :] = pair[0]
            w1[j, pl.ds(r, DEINT), :] = pair[1]
            return carry

        lax.fori_loop(0, FEAT // DEINT, body, 0, unroll=2)
        if o + 2 < NZ:
            stage_copy(o + 2).start()

    def project(half, o):
        x = xg[o, pl.ds(half * HALF, HALF), :]
        first = jnp.dot(x, w0[o], preferred_element_type=F32)
        if o == 0:
            acc[half, 0] = first
        else:
            acc[half, 0] += first

        @pl.when(s == 0)
        def _():
            second = jnp.dot(x, w1[shard_of(o)], preferred_element_type=F32)
            if o == 0:
                acc[half, 1] = second
            else:
                acc[half, 1] += second

    def kv_index(source, half):
        return half * NSEQ + source

    def kv_copy(src, source, half, which, device):
        return remote(
            src, kv.at[source, half], kv_send.at[half * 20 + which], kv_recv.at[kv_index(source, half)], device
        )

    def kv_wait(source, half):
        kv_copy(kv.at[source, half], source, half, 0, partner).wait_recv()

    def q_copy(half):
        rows = pl.ds(half * HALF, HALF)
        return remote(qs.at[rows], qbuf.at[rows], q_send.at[half], q_recv.at[half], across)

    def x_copies(half):
        return (
            kv_copy(kvs.at[half], q, half, 0, across),
            kv_copy(kvs.at[half], q, half, 1, across_other),
            kv_copy(kv.at[q, half], q, half, 2, same_other),
        )

    def finish(half):
        rows = pl.ds(half * HALF, HALF)

        @pl.when(s == 0)
        def _():
            lane = lax.broadcasted_iota(jnp.int32, (16, DH), 1)
            bias = jnp.where(lane < lengths[half], 0.0, NEG).astype(BF16)
            kvs[half, pl.ds(0, GROUP), :] = acc[half, 0, :, DH:].astype(BF16)
            kvs[half, pl.ds(GROUP, GROUP), :] = acc[half, 1, :, DH:].astype(BF16)
            kvs[half, pl.ds(2 * GROUP, 16), :] = bias
            kv[q, half, pl.ds(0, GROUP), :] = acc[half, 0, :, :DH].astype(BF16)
            kv[q, half, pl.ds(GROUP, GROUP), :] = acc[half, 1, :, :DH].astype(BF16)
            kv[q, half, pl.ds(2 * GROUP, 16), :] = bias
            for copy in x_copies(half):
                copy.start()

        @pl.when(s == 1)
        def _():
            scale = DH ** -0.5
            qs[rows, :] = acc[half, 0, :, :DH].astype(BF16) * jnp.asarray(scale, BF16)
            qbuf[rows, :] = acc[half, 0, :, DH:].astype(BF16) * jnp.asarray(scale, BF16)
            q_copy(half).start()

    def own_sources():
        return [seq_of(y, hh, c) for hh in (0, 1)]

    def y_sends(half):
        near = [(seq_of(y, hh, c), hh) for hh in (0, 1)]
        low = [(seq_of(y_down, hh, c), hh) for hh in (0, 1)]
        high = [(seq_of(y_up, hh, c), hh) for hh in (0, 1)]
        far = [(seq_of(y_far, hh, c), hh) for hh in (0, 1)]
        return near, low, high, far

    def forward(source, half, which, device):
        kv_copy(kv.at[source, half], source, half, which, device).start()

    def y_first(half):
        near, _, _, _ = y_sends(half)
        for source, hh in near:
            @pl.when(jnp.logical_or(s == 1, hh != xh))
            def _():
                kv_wait(source, half)
            forward(source, half, 3 + 2 * hh, up)
            forward(source, half, 4 + 2 * hh, down)
            forward(source, half, 9 + hh, partner)

    def y_second(half):
        _, low, high, _ = y_sends(half)
        (lo0, _), (lo1, _) = low
        (hi0, _), (hi1, _) = high
        kv_wait(lo0, half)
        forward(lo0, half, 7, up)
        forward(lo0, half, 11, partner)
        kv_wait(hi0, half)
        forward(hi0, half, 12, partner)
        kv_wait(hi1, half)
        forward(hi1, half, 8, down)
        forward(hi1, half, 13, partner)
        kv_wait(lo1, half)
        forward(lo1, half, 14, partner)

    def y_third(half):
        _, _, _, far = y_sends(half)
        for source, hh in far:
            kv_wait(source, half)
            forward(source, half, 15 + hh, partner)

    def shared_wait(half):
        for yy in (y, y_down, y_up, y_far):
            for hh in (0, 1):
                kv_wait(seq_of(yy, hh, 1 - c), half)

    TILE = 4

    def attend(half, begin, end):
        queries = qbuf[...]

        def tile(i, carry):
            best, total = carry
            b = i * TILE
            keys = jnp.concatenate([kv[b + j, half, pl.ds(0, GROUP), :] for j in range(TILE)], axis=0)
            values = jnp.concatenate([kv[b + j, half, pl.ds(GROUP, GROUP), :] for j in range(TILE)], axis=0)
            bias = jnp.concatenate(
                [kv[b + j, half, pl.ds(2 * GROUP, 16), pl.ds(0, GROUP)].astype(F32)[0:1] for j in range(TILE)], axis=1
            )
            scores = lax.dot_general(queries, keys, NT, preferred_element_type=F32) + bias
            new_best = jnp.maximum(best, jnp.max(scores, axis=1, keepdims=True))
            shrink = jnp.exp(best - new_best)
            probs = jnp.exp(scores - new_best).astype(BF16)
            total = total * shrink + jnp.sum(probs.astype(F32), axis=1, keepdims=True)
            oacc[...] = oacc[...] * shrink + jnp.dot(probs, values, preferred_element_type=F32)
            return new_best, total

        best, total = lax.fori_loop(begin, end, tile, (mx[:, 0:1], den[:, 0:1]))
        mx[:, 0:1] = best
        den[:, 0:1] = total

    part = xh * 2 + c

    def wo_x_copies():
        return (
            remote(w1.at[part], wo.at[part], wo_send.at[0], wo_recv.at[part], across),
            remote(w1.at[part], wo.at[part], wo_send.at[1], wo_recv.at[part], across_other),
        )

    def wo_share(hh):
        index = hh * 2 + c
        return remote(wo.at[index], wo.at[index], wo_send.at[2 + hh], wo_recv.at[index], partner)

    def wo_wait(index):
        remote(wo.at[index], wo.at[index], wo_send.at[0], wo_recv.at[index], partner).wait_recv()

    def wo_local():
        return pltpu.make_async_copy(w1.at[pl.ds(4, 4)], wo, load_sem.at[2])

    @pl.when(s == 0)
    def _():
        load_x(enc).wait()

    @pl.when(s == 1)
    def _():
        load_x(dec).wait()

    z_start(0)
    mx[...] = jnp.full_like(mx, NEG)
    den[...] = jnp.zeros_like(den)
    oacc[...] = jnp.zeros_like(oacc)
    split(0)
    project(0, 0)
    z_step(0, 1)
    z_start(1)
    split(1)
    project(0, 1)
    split(2)
    project(0, 2)
    z_step(0, 2)
    split(3)
    project(0, 3)
    split(4)
    project(0, 4)
    z_step(0, 3)
    z_step(1, 1)
    split(5)
    project(0, 5)
    split(6)
    project(0, 6)
    z_step(0, 4)
    z_step(1, 2)
    split(7)
    project(0, 7)
    finish(0)

    @pl.when(s == 1)
    def _():
        for copy in wo_x_copies():
            copy.start()
        wo_local().start()

    for o in (0, 1, 2):
        project(1, o)
    y_first(0)
    z_step(1, 3)
    project(1, 3)
    project(1, 4)
    y_second(0)
    z_step(1, 4)
    for o in (5, 6, 7):
        project(1, o)
    finish(1)
    y_third(0)

    @pl.when(s == 0)
    def _():
        q_copy(0).wait_recv()
        q_copy(1).wait_recv()

    y_first(1)
    shared_wait(0)
    attend(0, 0, 2)
    y_second(1)
    attend(0, 2, 4)
    y_third(1)

    @pl.when(s == 0)
    def _():
        for hh in (0, 1):
            wo_wait(hh * 2 + c)
            wo_share(hh).start()

    shared_wait(1)
    attend(1, 0, 4)

    att[s] = (oacc[...] / den[:, 0:1]).astype(BF16)
    att_copy = remote(att.at[s], att.at[s], at_send.at[0], at_recv.at[0], across)
    att_copy.start()

    @pl.when(s == 0)
    def _():
        for hh in (0, 1):
            wo_wait(hh * 2 + 1 - c)

    @pl.when(s == 1)
    def _():
        wo_local().wait()

    load_res.wait()
    remote(att.at[1 - s], att.at[1 - s], at_send.at[0], at_recv.at[0], across).wait_recv()

    def chunk(o):
        d = shard_of(o)
        block = wo[d // 2, pl.ds(pl.multiple_of((d % 2) * DH, DH), DH), :]
        pacc[o] = lax.dot_general(att[0], block[:, :DH], NT, preferred_element_type=F32) + lax.dot_general(
            att[1], block[:, DH:], NT, preferred_element_type=F32
        )

        @pl.when(jnp.logical_and(s == m // 4, d // 2 == m % 4))
        def _():
            columns = pl.ds(pl.multiple_of((d % 2) * DH, DH), DH)
            pacc[o] += dres[:, columns].astype(F32)

    def target(direction, distance):
        if distance == 0:
            return 0
        if distance == 4:
            return 7
        return 2 * distance - (0 if direction == "R" else 1)

    def rs_copy(stream, hop):
        k = STREAMS.index(stream) * 4 + hop
        return remote(sbuf.at[k], rbuf.at[k], rs_send.at[k], rs_recv.at[k], z_dev[stream[0]])

    def rs_start(stream):
        direction, sub = stream
        k = STREAMS.index(stream) * 4
        sbuf[k] = pacc[target(direction, REACH[stream]), pl.ds(sub * HALF, HALF), :].astype(BF16)
        rs_copy(stream, 0).start()

    def rs_step(stream, hop):
        direction, sub = stream
        k = STREAMS.index(stream) * 4 + hop
        rs_copy(stream, hop - 1).wait_recv()
        own = pacc[target(direction, REACH[stream] - hop), pl.ds(sub * HALF, HALF), :]
        sbuf[k] = (own + rbuf[k - 1].astype(F32)).astype(BF16)
        rs_copy(stream, hop).start()

    chunk(7)
    rs_start(("R", 0))
    rs_start(("L", 1))
    chunk(6)
    rs_start(("R", 1))
    chunk(5)
    rs_start(("L", 0))
    for o in (4, 3, 2, 1, 0):
        chunk(o)
    for hop in (1, 2, 3):
        for stream in STREAMS:
            if hop < REACH[stream]:
                rs_step(stream, hop)
    for sub in (0, 1):
        rows = pl.ds(sub * HALF, HALF)
        total = pacc[0, rows, :]
        for direction in ("R", "L"):
            stream = (direction, sub)
            k = STREAMS.index(stream) * 4 + REACH[stream] - 1
            rs_copy(stream, REACH[stream] - 1).wait_recv()
            total = total + rbuf[k].astype(F32)
        out[rows, :] = total.astype(BF16)

    for half in (0, 1):
        for stream in STREAMS:
            for distance in range(1, REACH[stream] + 1):
                z_copy(half, stream, distance).wait_send()
        for which in range(3, 17):
            kv_copy(kv.at[q, half], q, half, which, partner).wait_send()

    @pl.when(s == 0)
    def _():
        for half in (0, 1):
            for copy in x_copies(half):
                copy.wait_send()
        for hh in (0, 1):
            wo_share(hh).wait_send()

    @pl.when(s == 1)
    def _():
        for half in (0, 1):
            q_copy(half).wait_send()
        for copy in wo_x_copies():
            copy.wait_send()

    att_copy.wait_send()
    for stream in STREAMS:
        for hop in range(REACH[stream]):
            rs_copy(stream, hop).wait_send()


def local(enc_states, dec_states, section_weights, group_lengths):
    dma = pltpu.SemaphoreType.DMA
    vmem = pltpu.VMEM
    return pl.pallas_call(
        kernel,
        out_shape=jax.ShapeDtypeStruct((ROWS, DH), BF16),
        in_specs=[pl.BlockSpec(memory_space=pl.ANY)] * 3 + [pl.BlockSpec(memory_space=pltpu.SMEM)],
        out_specs=pl.BlockSpec(memory_space=pltpu.VMEM),
        scratch_shapes=[
            vmem((NZ, ROWS, FEAT), BF16),
            vmem((2, FEAT, 2, FEAT), BF16),
            vmem((NZ, FEAT, FEAT), BF16),
            vmem((NZ, FEAT, FEAT), BF16),
            vmem((4, FEAT, FEAT), BF16),
            vmem((2, 2, HALF, FEAT), F32),
            vmem((NSEQ, 2, BLOCK, DH), BF16),
            vmem((2, BLOCK, DH), BF16),
            vmem((ROWS, DH), BF16),
            vmem((ROWS, DH), BF16),
            vmem((ROWS, FEAT), BF16),
            vmem((2, ROWS, DH), BF16),
            vmem((ROWS, DH), F32),
            vmem((ROWS, 128), F32),
            vmem((ROWS, 128), F32),
            vmem((NZ, ROWS, DH), F32),
            vmem((16, HALF, DH), BF16),
            vmem((16, HALF, DH), BF16),
            dma((3,)),
            dma((2,)),
            dma((32,)),
            dma((32,)),
            dma((40,)),
            dma((32,)),
            dma((2,)),
            dma((2,)),
            dma((4,)),
            dma((4,)),
            dma((1,)),
            dma((1,)),
            dma((16,)),
            dma((16,)),
        ],
        compiler_params=pltpu.CompilerParams(
            collective_id=0, has_side_effects=True, vmem_limit_bytes=60 * 2**20
        ),
    )(enc_states, dec_states, section_weights, group_lengths)


def solution(mesh):
    in_specs = (P("seq", "mp"), P("seq", "mp"), P("segment", None, None, "mp"), P("seq"))
    out_specs = P("seq", ("segment", "mp"))
    return jax.shard_map(local, mesh=mesh, in_specs=in_specs, out_specs=out_specs, check_vma=False)
```

time: 329 us -> 86.8 us (0.26)
  waiting for transfers between devices: 233 us -> 0 us
  Pallas kernels: 0 us -> 83.8 us
  local copies, waits for them, and re-layouts: 39.8 us -> 1.57 us
  matrix products: 16.6 us -> 0 us
  between operations: 13.9 us -> 0.01 us
  blocking collectives: 13.2 us -> 0 us
  other arithmetic: 9.28 us -> 0 us
    all_gather x3 -> x0, waiting for transfers between devices: 139 us -> none  [the longest x1 60.6 us: local(): memory_piece = lax.all_gather(received, 'seq', axis=0, tiled=True)]
    pallas_call x0 -> x1, Pallas kernels: none -> 83.8 us  [local(): pl.pallas_call(kernel, out_shape=jax.ShapeDtypeStruct((ROWS, DH), BF16),...]
    reduce_scatter x1 -> x0, waiting for transfers between devices: 72.2 us -> none  [local(): lax.psum_scatter(term.astype(jnp.bfloat16), ('segment', 'mp'), scatter_di...]
    dynamic_slice x8 -> x0, local copies, waits for them, and re-layouts: 23.8 us -> none  [local(): carry, _ = lax.scan(one_block, carry, (memory_blocks, length_blocks))]
    ppermute x1 -> x0, waiting for transfers between devices: 19.8 us -> none  [from_behind(): lax.ppermute(value, axis, [(source, source + steps) for source in range(l...]
    dot_general x10 -> x0, matrix products: 16.6 us -> none  [the longest x1 5.51 us: output_term(): lax.dot_general(operand, local_weight[:, 1, :], (((1,), (1,)), ((), ())),...]
    unnamed x1 -> x0, blocking collectives: 13.2 us -> none
    unnamed x11 -> x1, local copies, waits for them, and re-layouts: 9.78 us -> 1.57 us
  transfers between devices with their start and end apart: 5 -> 0, of which waited for: 5 -> 0; matrix products, arithmetic and copies ran while one was open for 3% -> 0% of each run, Pallas kernels for 0% -> 0%
where the time goes in v1:
time: 86.8 us; the launch traced here: 85.3 us
  Pallas kernels  83.8 us (97%)
  local copies, waits for them, and re-layouts  1.57 us (2%)
    pallas_call x1, Pallas kernels, local(): pl.pallas_call(kernel, out_shape=jax.ShapeDtypeStruct((ROWS, DH), BF16),...  83.8 us

profile of v1, /device:TPU:2, one launch (start us, length us, event | category | flops | bytes accessed | tf_op | source)
XLA Modules:
  0.0 85.3 jit_solution(7052704999413093647)
XLA Ops:
  0.0 83.8 %shard_map.46 = bf16[256,256]{1,0:T(8,128)(2,1)} custom-call(bf16[256,512]{1,0:T(8,128)(2,1)} %enc.1, bf16[256,512]{1,0:T(8,128)(2,1)} %dec.1, bf16[1,4096,2,512]{3,2,1,0:T(2,128)(2,1)} %weights.1, s32[2]{0:T(128)} %lengths.1), custom_call_target="tpu_custom_call" | custom-call | tf_op jit(solution)/shard_map/pallas_call | solution.py:461
  83.8 1.6 %copy.6 = bf16[256,256]{1,0:T(8,128)(2,1)} copy(bf16[256,256]{1,0:T(8,128)(2,1)} %shard_map.46) | data formatting | bytes 262144

commit v2 on v1

--- a/solution.py
+++ b/solution.py
@@ -10,7 +10,7 @@
 DH, GROUP = 256, 128
 ROWS, FEAT, NZ, NSEQ = 256, 512, 8, 16
 HALF, QUART = ROWS // 2, ROWS // 4
-BLOCK = 2 * GROUP + 16
+VROWS = GROUP + 16
 NEG = -1e30
 DEINT = 32
 OFFSETS = (0, -1, 1, -2, 2, -3, 3, 4)
@@ -27,7 +27,7 @@
     return 2 * distance - (1 if direction == "R" else 0)
 
 
-def kernel(enc, dec, weights, lengths, out, xg, stage, w0, w1, wo, acc, kv, kvs, qbuf, qs, dres, att, oacc,
+def kernel(enc, dec, weights, lengths, out, xg, stage, w0, w1, wo, acc, kb, vb, ks, vs, qbuf, qs, dres, att, oacc,
            mx, den, pacc, sbuf, rbuf, load_sem, stage_sem, z_send, z_recv, kv_send, kv_recv, q_send, q_recv,
            wo_send, wo_recv, at_send, at_recv, rs_send, rs_recv):
     s = lax.axis_index("segment")
@@ -137,26 +137,34 @@
             else:
                 acc[half, 1] += second
 
-    def kv_index(source, half):
-        return half * NSEQ + source
-
-    def kv_copy(src, source, half, which, device):
+    def piece(source, half, p):
+        return kb.at[source, half] if p == 0 else vb.at[source, half]
+
+    def kv_copy(src, source, half, p, which, device):
         return remote(
-            src, kv.at[source, half], kv_send.at[half * 20 + which], kv_recv.at[kv_index(source, half)], device
-        )
-
-    def kv_wait(source, half):
-        kv_copy(kv.at[source, half], source, half, 0, partner).wait_recv()
+            src,
+            piece(source, half, p),
+            kv_send.at[(half * 2 + p) * 17 + which],
+            kv_recv.at[(half * 2 + p) * NSEQ + source],
+            device,
+        )
+
+    def kv_wait(source, half, p):
+        kv_copy(piece(source, half, p), source, half, p, 0, partner).wait_recv()
+
+    def forward(source, half, p, which, device):
+        kv_copy(piece(source, half, p), source, half, p, which, device).start()
 
     def q_copy(half):
         rows = pl.ds(half * HALF, HALF)
         return remote(qs.at[rows], qbuf.at[rows], q_send.at[half], q_recv.at[half], across)
 
-    def x_copies(half):
+    def x_copies(half, p):
+        other = ks.at[half] if p == 0 else vs.at[half]
         return (
-            kv_copy(kvs.at[half], q, half, 0, across),
-            kv_copy(kvs.at[half], q, half, 1, across_other),
-            kv_copy(kv.at[q, half], q, half, 2, same_other),
+            kv_copy(other, q, half, p, 0, across),
+            kv_copy(other, q, half, p, 1, across_other),
+            kv_copy(piece(q, half, p), q, half, p, 2, same_other),
         )
 
     def finish(half):
@@ -164,15 +172,17 @@
 
         @pl.when(s == 0)
         def _():
+            ks[half] = acc[half, 0, :, DH:].astype(BF16)
+            kb[q, half] = acc[half, 0, :, :DH].astype(BF16)
+            for copy in x_copies(half, 0):
+                copy.start()
             lane = lax.broadcasted_iota(jnp.int32, (16, DH), 1)
             bias = jnp.where(lane < lengths[half], 0.0, NEG).astype(BF16)
-            kvs[half, pl.ds(0, GROUP), :] = acc[half, 0, :, DH:].astype(BF16)
-            kvs[half, pl.ds(GROUP, GROUP), :] = acc[half, 1, :, DH:].astype(BF16)
-            kvs[half, pl.ds(2 * GROUP, 16), :] = bias
-            kv[q, half, pl.ds(0, GROUP), :] = acc[half, 0, :, :DH].astype(BF16)
-            kv[q, half, pl.ds(GROUP, GROUP), :] = acc[half, 1, :, :DH].astype(BF16)
-            kv[q, half, pl.ds(2 * GROUP, 16), :] = bias
-            for copy in x_copies(half):
+            vs[half, pl.ds(0, GROUP), :] = acc[half, 1, :, DH:].astype(BF16)
+            vs[half, pl.ds(GROUP, 16), :] = bias
+            vb[q, half, pl.ds(0, GROUP), :] = acc[half, 1, :, :DH].astype(BF16)
+            vb[q, half, pl.ds(GROUP, 16), :] = bias
+            for copy in x_copies(half, 1):
                 copy.start()
 
         @pl.when(s == 1)
@@ -182,79 +192,57 @@
             qbuf[rows, :] = acc[half, 0, :, DH:].astype(BF16) * jnp.asarray(scale, BF16)
             q_copy(half).start()
 
-    def own_sources():
-        return [seq_of(y, hh, c) for hh in (0, 1)]
-
-    def y_sends(half):
-        near = [(seq_of(y, hh, c), hh) for hh in (0, 1)]
-        low = [(seq_of(y_down, hh, c), hh) for hh in (0, 1)]
-        high = [(seq_of(y_up, hh, c), hh) for hh in (0, 1)]
-        far = [(seq_of(y_far, hh, c), hh) for hh in (0, 1)]
-        return near, low, high, far
-
-    def forward(source, half, which, device):
-        kv_copy(kv.at[source, half], source, half, which, device).start()
-
-    def y_first(half):
-        near, _, _, _ = y_sends(half)
-        for source, hh in near:
-            @pl.when(jnp.logical_or(s == 1, hh != xh))
-            def _():
-                kv_wait(source, half)
-            forward(source, half, 3 + 2 * hh, up)
-            forward(source, half, 4 + 2 * hh, down)
-            forward(source, half, 9 + hh, partner)
-
-    def y_second(half):
-        _, low, high, _ = y_sends(half)
-        (lo0, _), (lo1, _) = low
-        (hi0, _), (hi1, _) = high
-        kv_wait(lo0, half)
-        forward(lo0, half, 7, up)
-        forward(lo0, half, 11, partner)
-        kv_wait(hi0, half)
-        forward(hi0, half, 12, partner)
-        kv_wait(hi1, half)
-        forward(hi1, half, 8, down)
-        forward(hi1, half, 13, partner)
-        kv_wait(lo1, half)
-        forward(lo1, half, 14, partner)
-
-    def y_third(half):
-        _, _, _, far = y_sends(half)
-        for source, hh in far:
-            kv_wait(source, half)
-            forward(source, half, 15 + hh, partner)
-
-    def shared_wait(half):
-        for yy in (y, y_down, y_up, y_far):
-            for hh in (0, 1):
-                kv_wait(seq_of(yy, hh, 1 - c), half)
-
-    TILE = 4
-
-    def attend(half, begin, end):
-        queries = qbuf[...]
-
-        def tile(i, carry):
-            best, total = carry
-            b = i * TILE
-            keys = jnp.concatenate([kv[b + j, half, pl.ds(0, GROUP), :] for j in range(TILE)], axis=0)
-            values = jnp.concatenate([kv[b + j, half, pl.ds(GROUP, GROUP), :] for j in range(TILE)], axis=0)
-            bias = jnp.concatenate(
-                [kv[b + j, half, pl.ds(2 * GROUP, 16), pl.ds(0, GROUP)].astype(F32)[0:1] for j in range(TILE)], axis=1
-            )
-            scores = lax.dot_general(queries, keys, NT, preferred_element_type=F32) + bias
-            new_best = jnp.maximum(best, jnp.max(scores, axis=1, keepdims=True))
-            shrink = jnp.exp(best - new_best)
-            probs = jnp.exp(scores - new_best).astype(BF16)
-            total = total * shrink + jnp.sum(probs.astype(F32), axis=1, keepdims=True)
-            oacc[...] = oacc[...] * shrink + jnp.dot(probs, values, preferred_element_type=F32)
-            return new_best, total
-
-        best, total = lax.fori_loop(begin, end, tile, (mx[:, 0:1], den[:, 0:1]))
-        mx[:, 0:1] = best
-        den[:, 0:1] = total
+    def source_of(yy, k):
+        return seq_of(yy, xh if k == 0 else 1 - xh, c)
+
+    def y_near(half, k, local_source):
+        source = source_of(y, k)
+        for p in (0, 1):
+            if not local_source:
+                kv_wait(source, half, p)
+            forward(source, half, p, 3 + 2 * k, up)
+            forward(source, half, p, 4 + 2 * k, down)
+            forward(source, half, p, 8 + k, partner)
+
+    def y_next(half, k):
+        low, high = source_of(y_down, k), source_of(y_up, k)
+        kv_wait(low, half, 0)
+        forward(low, half, 0, 7 if k == 0 else 10, up)
+        forward(low, half, 0, 11 + k, partner)
+        kv_wait(high, half, 0)
+        forward(high, half, 0, 13 + k, partner)
+        kv_wait(high, half, 1)
+        forward(high, half, 1, 7 if k == 0 else 10, down)
+        forward(high, half, 1, 13 + k, partner)
+        kv_wait(low, half, 1)
+        forward(low, half, 1, 11 + k, partner)
+
+    def y_far_in(half, k):
+        source = source_of(y_far, k)
+        for p in (0, 1):
+            kv_wait(source, half, p)
+            forward(source, half, p, 15 + k, partner)
+
+    def shared_wait(half, yy):
+        for hh in (0, 1):
+            for p in (0, 1):
+                kv_wait(seq_of(yy, hh, 1 - c), half, p)
+
+    def attend(half, yy):
+        b = yy * 4
+        keys = jnp.concatenate([kb[b + j, half] for j in range(4)], axis=0)
+        values = jnp.concatenate([vb[b + j, half, pl.ds(0, GROUP), :] for j in range(4)], axis=0)
+        bias = jnp.concatenate(
+            [vb[b + j, half, pl.ds(GROUP, 16), pl.ds(0, GROUP)].astype(F32)[0:1] for j in range(4)], axis=1
+        )
+        best, total = mx[:, 0:1], den[:, 0:1]
+        scores = lax.dot_general(qbuf[...], keys, NT, preferred_element_type=F32) + bias
+        new_best = jnp.maximum(best, jnp.max(scores, axis=1, keepdims=True))
+        shrink = jnp.exp(best - new_best)
+        probs = jnp.exp(scores - new_best).astype(BF16)
+        mx[:, 0:1] = new_best
+        den[:, 0:1] = total * shrink + jnp.sum(probs.astype(F32), axis=1, keepdims=True)
+        oacc[...] = oacc[...] * shrink + jnp.dot(probs, values, preferred_element_type=F32)
 
     part = xh * 2 + c
 
@@ -281,6 +269,16 @@
     @pl.when(s == 1)
     def _():
         load_x(dec).wait()
+
+    def enc_side(body, *args):
+        @pl.when(s == 0)
+        def _():
+            body(*args)
+
+    def dec_side(body, *args):
+        @pl.when(s == 1)
+        def _():
+            body(*args)
 
     z_start(0)
     mx[...] = jnp.full_like(mx, NEG)
@@ -295,21 +293,22 @@
     split(2)
     project(0, 2)
     z_step(0, 2)
+    z_step(1, 1)
     split(3)
     project(0, 3)
     split(4)
     project(0, 4)
     z_step(0, 3)
-    z_step(1, 1)
+    z_step(1, 2)
     split(5)
     project(0, 5)
     split(6)
     project(0, 6)
+    split(7)
     z_step(0, 4)
-    z_step(1, 2)
-    split(7)
     project(0, 7)
     finish(0)
+    enc_side(y_near, 0, 0, True)
 
     @pl.when(s == 1)
     def _():
@@ -317,30 +316,42 @@
             copy.start()
         wo_local().start()
 
-    for o in (0, 1, 2):
+    z_step(1, 3)
+    for o in (0, 1, 2, 3, 4):
         project(1, o)
-    y_first(0)
-    z_step(1, 3)
-    project(1, 3)
-    project(1, 4)
-    y_second(0)
+    dec_side(y_near, 0, 0, False)
+    dec_side(y_near, 0, 1, False)
+    y_next(0, 0)
+    for o in (5, 6):
+        project(1, o)
     z_step(1, 4)
-    for o in (5, 6, 7):
-        project(1, o)
+    project(1, 7)
     finish(1)
-    y_third(0)
+    enc_side(y_near, 1, 0, True)
+    enc_side(y_near, 0, 1, False)
+    y_next(0, 1)
+    y_far_in(0, 0)
+    y_far_in(0, 1)
 
     @pl.when(s == 0)
     def _():
         q_copy(0).wait_recv()
         q_copy(1).wait_recv()
 
-    y_first(1)
-    shared_wait(0)
-    attend(0, 0, 2)
-    y_second(1)
-    attend(0, 2, 4)
-    y_third(1)
+    dec_side(y_near, 1, 0, False)
+    dec_side(y_near, 1, 1, False)
+    y_next(1, 0)
+    shared_wait(0, y)
+    attend(0, y)
+    enc_side(y_near, 1, 1, False)
+    shared_wait(0, y_down)
+    attend(0, y_down)
+    y_next(1, 1)
+    shared_wait(0, y_up)
+    attend(0, y_up)
+    shared_wait(0, y_far)
+    attend(0, y_far)
+    y_far_in(1, 0)
 
     @pl.when(s == 0)
     def _():
@@ -348,8 +359,15 @@
             wo_wait(hh * 2 + c)
             wo_share(hh).start()
 
-    shared_wait(1)
-    attend(1, 0, 4)
+    shared_wait(1, y)
+    attend(1, y)
+    y_far_in(1, 1)
+    shared_wait(1, y_down)
+    attend(1, y_down)
+    shared_wait(1, y_up)
+    attend(1, y_up)
+    shared_wait(1, y_far)
+    attend(1, y_far)
 
     att[s] = (oacc[...] / den[:, 0:1]).astype(BF16)
     att_copy = remote(att.at[s], att.at[s], at_send.at[0], at_recv.at[0], across)
@@ -431,14 +449,16 @@
         for stream in STREAMS:
             for distance in range(1, REACH[stream] + 1):
                 z_copy(half, stream, distance).wait_send()
-        for which in range(3, 17):
-            kv_copy(kv.at[q, half], q, half, which, partner).wait_send()
+        for p in (0, 1):
+            for which in range(3, 17):
+                kv_copy(piece(q, half, p), q, half, p, which, partner).wait_send()
 
     @pl.when(s == 0)
     def _():
         for half in (0, 1):
-            for copy in x_copies(half):
-                copy.wait_send()
+            for p in (0, 1):
+                for copy in x_copies(half, p):
+                    copy.wait_send()
         for hh in (0, 1):
             wo_share(hh).wait_send()
 
@@ -470,8 +490,10 @@
             vmem((NZ, FEAT, FEAT), BF16),
             vmem((4, FEAT, FEAT), BF16),
             vmem((2, 2, HALF, FEAT), F32),
-            vmem((NSEQ, 2, BLOCK, DH), BF16),
-            vmem((2, BLOCK, DH), BF16),
+            vmem((NSEQ, 2, GROUP, DH), BF16),
+            vmem((NSEQ, 2, VROWS, DH), BF16),
+            vmem((2, GROUP, DH), BF16),
+            vmem((2, VROWS, DH), BF16),
             vmem((ROWS, DH), BF16),
             vmem((ROWS, DH), BF16),
             vmem((ROWS, FEAT), BF16),
@@ -486,8 +508,8 @@
             dma((2,)),
             dma((32,)),
             dma((32,)),
-            dma((40,)),
-            dma((32,)),
+            dma((68,)),
+            dma((64,)),
             dma((2,)),
             dma((2,)),
             dma((4,)),

time: 86.8 us -> 81.5 us (0.939); the launches traced: 85.3 us -> 81.3 us
  Pallas kernels: 83.8 us -> 79.7 us
    pallas_call x1, Pallas kernels: 83.8 us -> 79.7 us  [local(): pl.pallas_call(kernel, out_shape=jax.ShapeDtypeStruct((ROWS, DH), BF16),...]
where the time goes in v2:
time: 81.5 us; the launch traced here: 81.3 us
  Pallas kernels  79.7 us (98%)
  local copies, waits for them, and re-layouts  1.57 us (2%)
    pallas_call x1, Pallas kernels, local(): pl.pallas_call(kernel, out_shape=jax.ShapeDtypeStruct((ROWS, DH), BF16),...  79.7 us

profile of v2, /device:TPU:2, one launch (start us, length us, event | category | flops | bytes accessed | tf_op | source)
XLA Modules:
  0.0 81.3 jit_solution(10024439157955636913)
XLA Ops:
  0.0 79.7 %shard_map.46 = bf16[256,256]{1,0:T(8,128)(2,1)} custom-call(bf16[256,512]{1,0:T(8,128)(2,1)} %enc.1, bf16[256,512]{1,0:T(8,128)(2,1)} %dec.1, bf16[1,4096,2,512]{3,2,1,0:T(2,128)(2,1)} %weights.1, s32[2]{0:T(128)} %lengths.1), custom_call_target="tpu_custom_call" | custom-call | tf_op jit(solution)/shard_map/pallas_call | solution.py:481
  79.8 1.6 %copy.6 = bf16[256,256]{1,0:T(8,128)(2,1)} copy(bf16[256,256]{1,0:T(8,128)(2,1)} %shard_map.46) | data formatting | bytes 262144

commit v3 on v2

--- a/solution.py
+++ b/solution.py
@@ -28,8 +28,8 @@
 
 
 def kernel(enc, dec, weights, lengths, out, xg, stage, w0, w1, wo, acc, kb, vb, ks, vs, qbuf, qs, dres, att, oacc,
-           mx, den, pacc, sbuf, rbuf, load_sem, stage_sem, z_send, z_recv, kv_send, kv_recv, q_send, q_recv,
-           wo_send, wo_recv, at_send, at_recv, rs_send, rs_recv):
+           mx, den, ps, psm, pr, prm, pacc, sbuf, rbuf, load_sem, stage_sem, z_send, z_recv, kv_send, kv_recv, q_send, q_recv,
+           wo_send, wo_recv, p_send, p_recv, rs_send, rs_recv):
     s = lax.axis_index("segment")
     q = lax.axis_index("seq")
     m = lax.axis_index("mp")
@@ -137,112 +137,137 @@
             else:
                 acc[half, 1] += second
 
-    def piece(source, half, p):
-        return kb.at[source, half] if p == 0 else vb.at[source, half]
-
-    def kv_copy(src, source, half, p, which, device):
+    def piece(index, half, p):
+        return kb.at[index, half] if p == 0 else vb.at[index, half]
+
+    def kv_copy(src, index, half, p, which, device):
         return remote(
             src,
-            piece(source, half, p),
-            kv_send.at[(half * 2 + p) * 17 + which],
-            kv_recv.at[(half * 2 + p) * NSEQ + source],
+            piece(index, half, p),
+            kv_send.at[(half * 2 + p) * 8 + which],
+            kv_recv.at[(half * 2 + p) * 8 + index],
             device,
         )
 
-    def kv_wait(source, half, p):
-        kv_copy(piece(source, half, p), source, half, p, 0, partner).wait_recv()
-
-    def forward(source, half, p, which, device):
-        kv_copy(piece(source, half, p), source, half, p, which, device).start()
-
-    def q_copy(half):
+    def kv_wait(index, half, p):
+        kv_copy(piece(index, half, p), index, half, p, 0, partner).wait_recv()
+
+    def forward(index, half, p, which, device):
+        kv_copy(piece(index, half, p), index, half, p, which, device).start()
+
+    def x_copy(half, p):
+        return kv_copy(ks.at[half] if p == 0 else vs.at[half], y * 2 + c, half, p, 0, across)
+
+    def q_copies(half):
         rows = pl.ds(half * HALF, HALF)
-        return remote(qs.at[rows], qbuf.at[rows], q_send.at[half], q_recv.at[half], across)
-
-    def x_copies(half, p):
-        other = ks.at[half] if p == 0 else vs.at[half]
         return (
-            kv_copy(other, q, half, p, 0, across),
-            kv_copy(other, q, half, p, 1, across_other),
-            kv_copy(piece(q, half, p), q, half, p, 2, same_other),
+            remote(qs.at[rows], qbuf.at[0, rows], q_send.at[half * 3], q_recv.at[half * 2], across),
+            remote(qs.at[rows], qbuf.at[1, rows], q_send.at[half * 3 + 1], q_recv.at[half * 2 + 1], across_other),
+            remote(qbuf.at[0, rows], qbuf.at[1, rows], q_send.at[half * 3 + 2], q_recv.at[half * 2 + 1], same_other),
         )
 
     def finish(half):
         rows = pl.ds(half * HALF, HALF)
+        own = y * 2 + c
 
         @pl.when(s == 0)
         def _():
             ks[half] = acc[half, 0, :, DH:].astype(BF16)
-            kb[q, half] = acc[half, 0, :, :DH].astype(BF16)
-            for copy in x_copies(half, 0):
-                copy.start()
+            x_copy(half, 0).start()
+            kb[own, half] = acc[half, 0, :, :DH].astype(BF16)
             lane = lax.broadcasted_iota(jnp.int32, (16, DH), 1)
             bias = jnp.where(lane < lengths[half], 0.0, NEG).astype(BF16)
             vs[half, pl.ds(0, GROUP), :] = acc[half, 1, :, DH:].astype(BF16)
             vs[half, pl.ds(GROUP, 16), :] = bias
-            vb[q, half, pl.ds(0, GROUP), :] = acc[half, 1, :, :DH].astype(BF16)
-            vb[q, half, pl.ds(GROUP, 16), :] = bias
-            for copy in x_copies(half, 1):
-                copy.start()
+            x_copy(half, 1).start()
+            vb[own, half, pl.ds(0, GROUP), :] = acc[half, 1, :, :DH].astype(BF16)
+            vb[own, half, pl.ds(GROUP, 16), :] = bias
 
         @pl.when(s == 1)
         def _():
             scale = DH ** -0.5
             qs[rows, :] = acc[half, 0, :, :DH].astype(BF16) * jnp.asarray(scale, BF16)
-            qbuf[rows, :] = acc[half, 0, :, DH:].astype(BF16) * jnp.asarray(scale, BF16)
-            q_copy(half).start()
-
-    def source_of(yy, k):
-        return seq_of(yy, xh if k == 0 else 1 - xh, c)
-
-    def y_near(half, k, local_source):
-        source = source_of(y, k)
+            qbuf[0, rows, :] = acc[half, 0, :, DH:].astype(BF16) * jnp.asarray(scale, BF16)
+            for copy in q_copies(half):
+                copy.start()
+
+    def y_near(half, local_source):
         for p in (0, 1):
             if not local_source:
-                kv_wait(source, half, p)
-            forward(source, half, p, 3 + 2 * k, up)
-            forward(source, half, p, 4 + 2 * k, down)
-            forward(source, half, p, 8 + k, partner)
-
-    def y_next(half, k):
-        low, high = source_of(y_down, k), source_of(y_up, k)
+                kv_wait(y * 2 + c, half, p)
+            forward(y * 2 + c, half, p, 1, up)
+            forward(y * 2 + c, half, p, 2, down)
+            forward(y * 2 + c, half, p, 3, partner)
+
+    def y_next(half):
+        low, high = y_down * 2 + c, y_up * 2 + c
         kv_wait(low, half, 0)
-        forward(low, half, 0, 7 if k == 0 else 10, up)
-        forward(low, half, 0, 11 + k, partner)
+        forward(low, half, 0, 4, up)
+        forward(low, half, 0, 5, partner)
         kv_wait(high, half, 0)
-        forward(high, half, 0, 13 + k, partner)
+        forward(high, half, 0, 6, partner)
         kv_wait(high, half, 1)
-        forward(high, half, 1, 7 if k == 0 else 10, down)
-        forward(high, half, 1, 13 + k, partner)
+        forward(high, half, 1, 4, down)
+        forward(high, half, 1, 6, partner)
         kv_wait(low, half, 1)
-        forward(low, half, 1, 11 + k, partner)
-
-    def y_far_in(half, k):
-        source = source_of(y_far, k)
+        forward(low, half, 1, 5, partner)
+
+    def y_last(half):
         for p in (0, 1):
-            kv_wait(source, half, p)
-            forward(source, half, p, 15 + k, partner)
-
-    def shared_wait(half, yy):
-        for hh in (0, 1):
+            kv_wait(y_far * 2 + c, half, p)
+            forward(y_far * 2 + c, half, p, 7, partner)
+
+    def shared_wait(half, *positions):
+        for yy in positions:
             for p in (0, 1):
-                kv_wait(seq_of(yy, hh, 1 - c), half, p)
-
-    def attend(half, yy):
-        b = yy * 4
-        keys = jnp.concatenate([kb[b + j, half] for j in range(4)], axis=0)
-        values = jnp.concatenate([vb[b + j, half, pl.ds(0, GROUP), :] for j in range(4)], axis=0)
+                kv_wait(yy * 2 + 1 - c, half, p)
+
+    def attend(half, first, second, k):
+        blocks = (first * 2, first * 2 + 1, second * 2, second * 2 + 1)
+        keys = jnp.concatenate([kb[b, half] for b in blocks], axis=0)
+        values = jnp.concatenate([vb[b, half, pl.ds(0, GROUP), :] for b in blocks], axis=0)
         bias = jnp.concatenate(
-            [vb[b + j, half, pl.ds(GROUP, 16), pl.ds(0, GROUP)].astype(F32)[0:1] for j in range(4)], axis=1
-        )
-        best, total = mx[:, 0:1], den[:, 0:1]
-        scores = lax.dot_general(qbuf[...], keys, NT, preferred_element_type=F32) + bias
+            [vb[b, half, pl.ds(GROUP, 16), pl.ds(0, GROUP)].astype(F32)[0:1] for b in blocks], axis=1
+        )
+        best, total = mx[k, :, 0:1], den[k, :, 0:1]
+        scores = lax.dot_general(qbuf[k], keys, NT, preferred_element_type=F32) + bias
         new_best = jnp.maximum(best, jnp.max(scores, axis=1, keepdims=True))
         shrink = jnp.exp(best - new_best)
         probs = jnp.exp(scores - new_best).astype(BF16)
-        mx[:, 0:1] = new_best
-        den[:, 0:1] = total * shrink + jnp.sum(probs.astype(F32), axis=1, keepdims=True)
-        oacc[...] = oacc[...] * shrink + jnp.dot(probs, values, preferred_element_type=F32)
+        mx[k] = jnp.broadcast_to(new_best, (ROWS, 128))
+        den[k] = jnp.broadcast_to(total * shrink + jnp.sum(probs.astype(F32), axis=1, keepdims=True), (ROWS, 128))
+        oacc[k] = oacc[k] * shrink + jnp.dot(probs, values, preferred_element_type=F32)
+
+    def part_copies(k, device):
+        return (
+            remote(ps.at[k], pr.at[k], p_send.at[2 * k], p_recv.at[2 * k], device),
+            remote(psm.at[k], prm.at[k], p_send.at[2 * k + 1], p_recv.at[2 * k + 1], device),
+        )
+
+    def part_send(k):
+        ps[k] = oacc[k].astype(BF16)
+        psm[k, pl.ds(0, 8), :] = jnp.transpose(mx[k])[0:8]
+        psm[k, pl.ds(8, 8), :] = jnp.transpose(den[k])[0:8]
+        for copy in part_copies(k, across if k == 0 else across_other):
+            copy.start()
+
+    def relay_copies():
+        return (
+            remote(pr.at[1], pr.at[2], p_send.at[4], p_recv.at[4], across),
+            remote(prm.at[1], prm.at[2], p_send.at[5], p_recv.at[5], across),
+        )
+
+    def column(row):
+        return jnp.transpose(jnp.broadcast_to(row, (128, ROWS)))[:, 0:1]
+
+    def merge(head, one, one_best, one_sum, two, two_best, two_sum):
+        best = jnp.maximum(one_best, two_best)
+        one_share, two_share = jnp.exp(one_best - best), jnp.exp(two_best - best)
+        scale = 1.0 / (one_sum * one_share + two_sum * two_share)
+        att[head] = (one * (one_share * scale) + two * (two_share * scale)).astype(BF16)
+
+    def received(slot):
+        return pr[slot].astype(F32), column(prm[slot, 0:1, :]), column(prm[slot, 8:9, :])
 
     part = xh * 2 + c
 
@@ -308,7 +333,7 @@
     z_step(0, 4)
     project(0, 7)
     finish(0)
-    enc_side(y_near, 0, 0, True)
+    enc_side(y_near, 0, True)
 
     @pl.when(s == 1)
     def _():
@@ -319,39 +344,31 @@
     z_step(1, 3)
     for o in (0, 1, 2, 3, 4):
         project(1, o)
-    dec_side(y_near, 0, 0, False)
-    dec_side(y_near, 0, 1, False)
-    y_next(0, 0)
+    dec_side(y_near, 0, False)
+    y_next(0)
     for o in (5, 6):
         project(1, o)
     z_step(1, 4)
     project(1, 7)
     finish(1)
-    enc_side(y_near, 1, 0, True)
-    enc_side(y_near, 0, 1, False)
-    y_next(0, 1)
-    y_far_in(0, 0)
-    y_far_in(0, 1)
+    enc_side(y_near, 1, True)
+    y_last(0)
+    for half in (0, 1):
+        q_copies(half)[1].wait_recv()
 
     @pl.when(s == 0)
     def _():
-        q_copy(0).wait_recv()
-        q_copy(1).wait_recv()
-
-    dec_side(y_near, 1, 0, False)
-    dec_side(y_near, 1, 1, False)
-    y_next(1, 0)
-    shared_wait(0, y)
-    attend(0, y)
-    enc_side(y_near, 1, 1, False)
-    shared_wait(0, y_down)
-    attend(0, y_down)
-    y_next(1, 1)
-    shared_wait(0, y_up)
-    attend(0, y_up)
-    shared_wait(0, y_far)
-    attend(0, y_far)
-    y_far_in(1, 0)
+        for half in (0, 1):
+            q_copies(half)[0].wait_recv()
+
+    shared_wait(0, y, y_down)
+    attend(0, y, y_down, 1)
+    attend(0, y, y_down, 0)
+    dec_side(y_near, 1, False)
+    shared_wait(0, y_up, y_far)
+    attend(0, y_up, y_far, 1)
+    attend(0, y_up, y_far, 0)
+    y_next(1)
 
     @pl.when(s == 0)
     def _():
@@ -359,19 +376,15 @@
             wo_wait(hh * 2 + c)
             wo_share(hh).start()
 
-    shared_wait(1, y)
-    attend(1, y)
-    y_far_in(1, 1)
-    shared_wait(1, y_down)
-    attend(1, y_down)
-    shared_wait(1, y_up)
-    attend(1, y_up)
-    shared_wait(1, y_far)
-    attend(1, y_far)
-
-    att[s] = (oacc[...] / den[:, 0:1]).astype(BF16)
-    att_copy = remote(att.at[s], att.at[s], at_send.at[0], at_recv.at[0], across)
-    att_copy.start()
+    y_last(1)
+    shared_wait(1, y, y_down)
+    attend(1, y, y_down, 1)
+    attend(1, y, y_down, 0)
+    shared_wait(1, y_up, y_far)
+    attend(1, y_up, y_far, 1)
+    part_send(1)
+    attend(1, y_up, y_far, 0)
+    part_send(0)
 
     @pl.when(s == 0)
     def _():
@@ -383,7 +396,16 @@
         wo_local().wait()
 
     load_res.wait()
-    remote(att.at[1 - s], att.at[1 - s], at_send.at[0], at_recv.at[0], across).wait_recv()
+    for copy in part_copies(1, across_other):
+        copy.wait_recv()
+    for copy in relay_copies():
+        copy.start()
+    for copy in part_copies(0, across):
+        copy.wait_recv()
+    merge(1 - s, *received(0), *received(1))
+    for copy in relay_copies():
+        copy.wait_recv()
+    merge(s, oacc[0], mx[0, :, 0:1], den[0, :, 0:1], *received(2))
 
     def chunk(o):
         d = shard_of(o)
@@ -450,26 +472,27 @@
             for distance in range(1, REACH[stream] + 1):
                 z_copy(half, stream, distance).wait_send()
         for p in (0, 1):
-            for which in range(3, 17):
-                kv_copy(piece(q, half, p), q, half, p, which, partner).wait_send()
+            for which in range(1, 8):
+                kv_copy(piece(0, half, p), 0, half, p, which, partner).wait_send()
 
     @pl.when(s == 0)
     def _():
         for half in (0, 1):
             for p in (0, 1):
-                for copy in x_copies(half, p):
-                    copy.wait_send()
+                x_copy(half, p).wait_send()
         for hh in (0, 1):
             wo_share(hh).wait_send()
 
     @pl.when(s == 1)
     def _():
         for half in (0, 1):
-            q_copy(half).wait_send()
+            for copy in q_copies(half):
+                copy.wait_send()
         for copy in wo_x_copies():
             copy.wait_send()
 
-    att_copy.wait_send()
+    for copy in (*part_copies(0, across), *part_copies(1, across_other), *relay_copies()):
+        copy.wait_send()
     for stream in STREAMS:
         for hop in range(REACH[stream]):
             rs_copy(stream, hop).wait_send()
@@ -490,17 +513,21 @@
             vmem((NZ, FEAT, FEAT), BF16),
             vmem((4, FEAT, FEAT), BF16),
             vmem((2, 2, HALF, FEAT), F32),
-            vmem((NSEQ, 2, GROUP, DH), BF16),
-            vmem((NSEQ, 2, VROWS, DH), BF16),
+            vmem((8, 2, GROUP, DH), BF16),
+            vmem((8, 2, VROWS, DH), BF16),
             vmem((2, GROUP, DH), BF16),
             vmem((2, VROWS, DH), BF16),
-            vmem((ROWS, DH), BF16),
+            vmem((2, ROWS, DH), BF16),
             vmem((ROWS, DH), BF16),
             vmem((ROWS, FEAT), BF16),
             vmem((2, ROWS, DH), BF16),
-            vmem((ROWS, DH), F32),
-            vmem((ROWS, 128), F32),
-            vmem((ROWS, 128), F32),
+            vmem((2, ROWS, DH), F32),
+            vmem((2, ROWS, 128), F32),
+            vmem((2, ROWS, 128), F32),
+            vmem((2, ROWS, DH), BF16),
+            vmem((2, 16, ROWS), F32),
+            vmem((3, ROWS, DH), BF16),
+            vmem((3, 16, ROWS), F32),
             vmem((NZ, ROWS, DH), F32),
             vmem((16, HALF, DH), BF16),
             vmem((16, HALF, DH), BF16),
@@ -508,14 +535,14 @@
             dma((2,)),
             dma((32,)),
             dma((32,)),
-            dma((68,)),
-            dma((64,)),
-            dma((2,)),
-            dma((2,)),
+            dma((32,)),
+            dma((32,)),
+            dma((6,)),
             dma((4,)),
             dma((4,)),
-            dma((1,)),
-            dma((1,)),
+            dma((4,)),
+            dma((6,)),
+            dma((6,)),
             dma((16,)),
             dma((16,)),
         ],

time: 81.5 us -> 84.8 us (1.040)
  Pallas kernels: 79.7 us -> 83.1 us
    pallas_call x1, Pallas kernels: 79.7 us -> 83.1 us  [local(): pl.pallas_call(kernel, out_shape=jax.ShapeDtypeStruct((ROWS, DH), BF16),...]
where the time goes in v3:
time: 84.8 us; the launch traced here: 84.7 us
  Pallas kernels  83.1 us (98%)
  local copies, waits for them, and re-layouts  1.57 us (2%)
    pallas_call x1, Pallas kernels, local(): pl.pallas_call(kernel, out_shape=jax.ShapeDtypeStruct((ROWS, DH), BF16),...  83.1 us

profile of v3, /device:TPU:2, one launch (start us, length us, event | category | flops | bytes accessed | tf_op | source)
XLA Modules:
  0.0 84.7 jit_solution(10798809725295121005)
XLA Ops:
  0.0 83.1 %shard_map.46 = bf16[256,256]{1,0:T(8,128)(2,1)} custom-call(bf16[256,512]{1,0:T(8,128)(2,1)} %enc.1, bf16[256,512]{1,0:T(8,128)(2,1)} %dec.1, bf16[1,4096,2,512]{3,2,1,0:T(2,128)(2,1)} %weights.1, s32[2]{0:T(128)} %lengths.1), custom_call_target="tpu_custom_call" | custom-call | tf_op jit(solution)/shard_map/pallas_call | solution.py:504
  83.1 1.6 %copy.6 = bf16[256,256]{1,0:T(8,128)(2,1)} copy(bf16[256,256]{1,0:T(8,128)(2,1)} %shard_map.46) | data formatting | bytes 262144

commit v4 on v3

v4 whole, which is shorter than its diff:
```python
import jax
import jax.numpy as jnp
from jax import lax
from jax.experimental import pallas as pl
from jax.experimental.pallas import tpu as pltpu
from jax.sharding import PartitionSpec as P

MESH = pl.DeviceIdType.MESH
F32, BF16 = jnp.float32, jnp.bfloat16
DH, GROUP = 256, 128
ROWS, FEAT, NZ = 256, 512, 8
HALF, QUART = ROWS // 2, ROWS // 4
BLOCK = 2 * (GROUP // 2) + 16
NEG = -1e30
DEINT = 32
OFFSETS = (0, -1, 1, -2, 2, -3, 3, 4)
REACH = {("R", 0): 4, ("R", 1): 3, ("L", 1): 4, ("L", 0): 3}
QUARTERS = (0, 1, 2, 3)
STREAMS = (("R", 0), ("L", 1), ("R", 1), ("L", 0))
NT = (((1,), (1,)), ((), ()))


def slot_of(direction, distance):
    if distance == 0:
        return 0
    if distance == 4:
        return 7
    return 2 * distance - (1 if direction == "R" else 0)


def kernel(enc, dec, weights, lengths, out, xg, stage, w0, w1, wo, acc, kv, ks, qbuf, qs, dres, att, oacc,
           mx, den, ps, psm, pr, prm, pacc, sbuf, rbuf, load_sem, stage_sem, z_send, z_recv, kv_send, kv_recv, q_send, q_recv,
           wo_send, wo_recv, p_send, p_recv, rs_send, rs_recv):
    s = lax.axis_index("segment")
    q = lax.axis_index("seq")
    m = lax.axis_index("mp")
    y, xh, c = q // 4, (q // 2) % 2, q % 2
    z_to = {"R": (m + 1) % NZ, "L": (m + NZ - 1) % NZ}

    def seq_of(yy, hh, cc):
        return (yy * 2 + hh) * 2 + cc

    y_up, y_down, y_far = (y + 1) % 4, (y + 3) % 4, (y + 2) % 4
    partner = (s, seq_of(y, xh, 1 - c), m)
    up, down = (s, seq_of(y_up, xh, c), m), (s, seq_of(y_down, xh, c), m)
    across = (1 - s, q, m)
    across_other = (1 - s, seq_of(y, 1 - xh, c), m)
    same_other = (s, seq_of(y, 1 - xh, c), m)
    z_dev = {d: (s, q, z_to[d]) for d in ("R", "L")}

    def remote(src, dst, send, recv, device):
        return pltpu.make_async_remote_copy(
            src_ref=src, dst_ref=dst, send_sem=send, recv_sem=recv, device_id=device, device_id_type=MESH
        )

    def load_x(source):
        return pltpu.make_async_copy(source, xg.at[0], load_sem.at[0])

    @pl.when(s == 0)
    def _():
        load_x(enc).start()

    @pl.when(s == 1)
    def _():
        load_x(dec).start()

    load_res = pltpu.make_async_copy(dec, dres, load_sem.at[1])
    load_res.start()

    def shard_of(o):
        return (m + NZ + OFFSETS[o]) % NZ

    def stage_copy(o):
        rows = pl.ds(pl.multiple_of(shard_of(o) * FEAT, FEAT), FEAT)
        return pltpu.make_async_copy(weights.at[0, rows], stage.at[o % 2], stage_sem.at[o % 2])

    stage_copy(0).start()
    stage_copy(1).start()

    barrier = pltpu.get_barrier_semaphore()
    peers = (z_dev["R"], z_dev["L"], up, down, partner, across, across_other, same_other)
    for peer in peers:
        pl.semaphore_signal(barrier, inc=1, device_id=peer, device_id_type=MESH)
    pl.semaphore_wait(barrier, len(peers))

    def z_copy(r, direction, distance):
        rows = pl.ds(r * QUART, QUART)
        sems = (r * 2 + (direction == "L")) * 4 + distance - 1
        return remote(
            xg.at[slot_of(direction, distance - 1), rows],
            xg.at[slot_of(direction, distance), rows],
            z_send.at[sems],
            z_recv.at[sems],
            z_dev[direction],
        )

    def z_start(*quarters):
        for r in quarters:
            for direction in ("R", "L"):
                z_copy(r, direction, 1).start()

    def z_step(r, distance):
        for direction in ("R", "L"):
            reach = REACH[direction, r % 2]
            if distance <= reach:
                z_copy(r, direction, distance).wait_recv()
                if distance < reach:
                    z_copy(r, direction, distance + 1).start()

    def split(o):
        stage_copy(o).wait()
        j = shard_of(o)

        def body(i, carry):
            r = pl.multiple_of(i * DEINT, DEINT)
            pair = jnp.swapaxes(stage[o % 2, pl.ds(r, DEINT)], 0, 1)
            w0[o, pl.ds(r, DEINT), :] = pair[0]
            w1[j, pl.ds(r, DEINT), :] = pair[1]
            return carry

        lax.fori_loop(0, FEAT // DEINT, body, 0, unroll=2)
        if o + 2 < NZ:
            stage_copy(o + 2).start()

    def project(begin, end, o):
        rows = pl.ds(begin * QUART, (end - begin) * QUART)
        x = xg[o, rows, :]
        first = jnp.dot(x, w0[o], preferred_element_type=F32)
        if o == 0:
            acc[0, rows, :] = first
        else:
            acc[0, rows, :] += first

        @pl.when(s == 0)
        def _():
            second = jnp.dot(x, w1[shard_of(o)], preferred_element_type=F32)
            if o == 0:
                acc[1, rows, :] = second
            else:
                acc[1, rows, :] += second

    def kv_copy(src, index, r, which, device):
        return remote(src, kv.at[index, r], kv_send.at[r * 8 + which], kv_recv.at[r * 8 + index], device)

    def kv_wait(index, r):
        kv_copy(kv.at[index, r], index, r, 0, partner).wait_recv()

    def forward(index, r, which, device):
        kv_copy(kv.at[index, r], index, r, which, device).start()

    def x_copy(r):
        return kv_copy(ks.at[r], y * 2 + c, r, 0, across)

    def q_copies(r):
        rows = pl.ds(r * QUART, QUART)
        return (
            remote(qs.at[rows], qbuf.at[0, rows], q_send.at[r * 3], q_recv.at[r * 2], across),
            remote(qs.at[rows], qbuf.at[1, rows], q_send.at[r * 3 + 1], q_recv.at[r * 2 + 1], across_other),
            remote(qbuf.at[0, rows], qbuf.at[1, rows], q_send.at[r * 3 + 2], q_recv.at[r * 2 + 1], same_other),
        )

    def finish(r):
        rows = pl.ds(r * QUART, QUART)
        own = y * 2 + c

        @pl.when(s == 0)
        def _():
            lane = lax.broadcasted_iota(jnp.int32, (16, DH), 1) - c * QUART
            padding = jnp.logical_and(lane >= 0, lane + (r % 2) * QUART >= lengths[r // 2])
            bias = jnp.where(jnp.logical_and(padding, lane < QUART), NEG, 0.0).astype(BF16)
            ks[r, pl.ds(0, QUART), :] = acc[0, rows, DH:].astype(BF16)
            ks[r, pl.ds(QUART, QUART), :] = acc[1, rows, DH:].astype(BF16)
            ks[r, pl.ds(2 * QUART, 16), :] = bias
            x_copy(r).start()
            kv[own, r, pl.ds(0, QUART), :] = acc[0, rows, :DH].astype(BF16)
            kv[own, r, pl.ds(QUART, QUART), :] = acc[1, rows, :DH].astype(BF16)
            kv[own, r, pl.ds(2 * QUART, 16), :] = bias
            y_near(r, True)

        @pl.when(s == 1)
        def _():
            scale = DH ** -0.5
            qs[rows, :] = acc[0, rows, :DH].astype(BF16) * jnp.asarray(scale, BF16)
            qbuf[0, rows, :] = acc[0, rows, DH:].astype(BF16) * jnp.asarray(scale, BF16)
            for copy in q_copies(r):
                copy.start()

    def y_near(r, local_source):
        index = y * 2 + c
        if not local_source:
            kv_wait(index, r)
        forward(index, r, 1, up)
        forward(index, r, 2, down)
        forward(index, r, 3, partner)

    def y_next(r):
        low, high = y_down * 2 + c, y_up * 2 + c
        one, other = ((low, up, 5, 6), high) if r % 2 == 0 else ((high, down, 6, 5), low)
        index, device, share_one, share_other = one
        kv_wait(index, r)
        forward(index, r, 4, device)
        forward(index, r, share_one, partner)
        kv_wait(other, r)
        forward(other, r, share_other, partner)

    def y_last(r):
        kv_wait(y_far * 2 + c, r)
        forward(y_far * 2 + c, r, 7, partner)

    def shared_wait(r):
        for yy in (y, y_down, y_up, y_far):
            kv_wait(yy * 2 + 1 - c, r)

    def attend(r, k):
        keys = jnp.concatenate([kv[b, r, pl.ds(0, QUART), :] for b in range(8)], axis=0)
        values = jnp.concatenate([kv[b, r, pl.ds(QUART, QUART), :] for b in range(8)], axis=0)
        signs = [kv[b, r, pl.ds(2 * QUART, 16), pl.ds(0, GROUP)].astype(F32)[0:1] for b in range(8)]
        bias = jnp.concatenate([signs[b] + signs[b + 1] for b in range(0, 8, 2)], axis=1)
        best, total = mx[k, :, 0:1], den[k, :, 0:1]
        scores = lax.dot_general(qbuf[k], keys, NT, preferred_element_type=F32) + bias
        new_best = jnp.maximum(best, jnp.max(scores, axis=1, keepdims=True))
        shrink = jnp.exp(best - new_best)
        probs = jnp.exp(scores - new_best).astype(BF16)
        mx[k] = jnp.broadcast_to(new_best, (ROWS, 128))
        den[k] = jnp.broadcast_to(total * shrink + jnp.sum(probs.astype(F32), axis=1, keepdims=True), (ROWS, 128))
        oacc[k] = oacc[k] * shrink + jnp.dot(probs, values, preferred_element_type=F32)

    def part_copies(k, g, device):
        rows = pl.ds(g * HALF, HALF)
        sems = (k * 2 + g) * 2
        return (
            remote(ps.at[k, rows], pr.at[k, rows], p_send.at[sems], p_recv.at[sems], device),
            remote(psm.at[k, g], prm.at[k, g], p_send.at[sems + 1], p_recv.at[sems + 1], device),
        )

    def part_send(k):
        for g in (0, 1):
            rows = pl.ds(g * HALF, HALF)
            ps[k, rows, :] = oacc[k, rows, :].astype(BF16)
            psm[k, g, pl.ds(0, 8), :] = jnp.transpose(mx[k, rows, :])[0:8]
            psm[k, g, pl.ds(8, 8), :] = jnp.transpose(den[k, rows, :])[0:8]
            for copy in part_copies(k, g, across if k == 0 else across_other):
                copy.start()

    def relay_copies(g):
        rows = pl.ds(g * HALF, HALF)
        sems = 8 + 2 * g
        return (
            remote(pr.at[1, rows], pr.at[2, rows], p_send.at[sems], p_recv.at[sems], across),
            remote(prm.at[1, g], prm.at[2, g], p_send.at[sems + 1], p_recv.at[sems + 1], across),
        )

    def column(row):
        return jnp.transpose(jnp.broadcast_to(row, (128, HALF)))[:, 0:1]

    def merge(head, g, one, one_best, one_sum, two, two_best, two_sum):
        best = jnp.maximum(one_best, two_best)
        one_share, two_share = jnp.exp(one_best - best), jnp.exp(two_best - best)
        scale = 1.0 / (one_sum * one_share + two_sum * two_share)
        att[head, pl.ds(g * HALF, HALF), :] = (one * (one_share * scale) + two * (two_share * scale)).astype(BF16)

    def received(slot, g):
        rows = pl.ds(g * HALF, HALF)
        return pr[slot, rows, :].astype(F32), column(prm[slot, g, 0:1, :]), column(prm[slot, g, 8:9, :])

    def part_wait(copies):
        for copy in copies:
            copy.wait_recv()

    part = xh * 2 + c

    def wo_x_copies():
        return (
            remote(w1.at[part], wo.at[part], wo_send.at[0], wo_recv.at[part], across),
            remote(w1.at[part], wo.at[part], wo_send.at[1], wo_recv.at[part], across_other),
        )

    def wo_share(hh):
        index = hh * 2 + c
        return remote(wo.at[index], wo.at[index], wo_send.at[2 + hh], wo_recv.at[index], partner)

    def wo_wait(index):
        remote(wo.at[index], wo.at[index], wo_send.at[0], wo_recv.at[index], partner).wait_recv()

    def wo_local():
        return pltpu.make_async_copy(w1.at[pl.ds(4, 4)], wo, load_sem.at[2])

    @pl.when(s == 0)
    def _():
        load_x(enc).wait()

    @pl.when(s == 1)
    def _():
        load_x(dec).wait()

    def enc_side(body, *args):
        @pl.when(s == 0)
        def _():
            body(*args)

    def dec_side(body, *args):
        @pl.when(s == 1)
        def _():
            body(*args)

    z_start(0, 1, 2)
    mx[...] = jnp.full_like(mx, NEG)
    den[...] = jnp.zeros_like(den)
    oacc[...] = jnp.zeros_like(oacc)
    split(0)
    project(0, 2, 0)
    z_step(0, 1)
    z_step(1, 1)
    z_start(3)
    split(1)
    project(0, 2, 1)
    split(2)
    project(0, 2, 2)
    z_step(2, 1)
    z_step(0, 2)
    z_step(1, 2)
    split(3)
    project(0, 2, 3)
    split(4)
    project(0, 2, 4)
    z_step(3, 1)
    z_step(2, 2)
    z_step(0, 3)
    z_step(1, 3)
    split(5)
    project(0, 2, 5)
    split(6)
    project(0, 2, 6)
    split(7)
    z_step(2, 3)
    z_step(3, 2)
    z_step(0, 4)
    z_step(1, 4)
    project(0, 2, 7)
    finish(0)
    finish(1)

    @pl.when(s == 1)
    def _():
        for copy in wo_x_copies():
            copy.start()
        wo_local().start()

    for o in range(7):
        project(2, 3, o)
    z_step(2, 4)
    z_step(3, 3)
    project(2, 3, 7)
    finish(2)
    for o in range(7):
        project(3, 4, o)
    dec_side(y_near, 0, False)
    dec_side(y_near, 1, False)
    z_step(3, 4)
    project(3, 4, 7)
    finish(3)
    y_next(0)
    dec_side(y_near, 2, False)
    y_next(1)
    dec_side(y_near, 3, False)
    y_next(2)
    y_last(0)
    y_last(1)
    for r in QUARTERS:
        q_copies(r)[1].wait_recv()

    @pl.when(s == 0)
    def _():
        for r in QUARTERS:
            q_copies(r)[0].wait_recv()

    shared_wait(0)
    attend(0, 1)
    attend(0, 0)
    y_next(3)
    shared_wait(1)
    attend(1, 1)
    y_last(2)
    attend(1, 0)
    y_last(3)
    shared_wait(2)
    attend(2, 1)
    attend(2, 0)

    @pl.when(s == 0)
    def _():
        for hh in (0, 1):
            wo_wait(hh * 2 + c)
            wo_share(hh).start()

    shared_wait(3)
    attend(3, 1)
    part_send(1)
    attend(3, 0)
    part_send(0)

    @pl.when(s == 0)
    def _():
        for hh in (0, 1):
            wo_wait(hh * 2 + 1 - c)

    @pl.when(s == 1)
    def _():
        wo_local().wait()

    load_res.wait()

    def chunk(o, g):
        rows = pl.ds(g * HALF, HALF)
        d = shard_of(o)
        block = wo[d // 2, pl.ds(pl.multiple_of((d % 2) * DH, DH), DH), :]
        pacc[o, rows, :] = lax.dot_general(
            att[0, rows, :], block[:, :DH], NT, preferred_element_type=F32
        ) + lax.dot_general(att[1, rows, :], block[:, DH:], NT, preferred_element_type=F32)

        @pl.when(jnp.logical_and(s == m // 4, d // 2 == m % 4))
        def _():
            columns = pl.ds(pl.multiple_of((d % 2) * DH, DH), DH)
            pacc[o, rows, :] += dres[rows, columns].astype(F32)

    def target(direction, distance):
        if distance == 0:
            return 0
        if distance == 4:
            return 7
        return 2 * distance - (0 if direction == "R" else 1)

    def rs_copy(stream, hop):
        k = STREAMS.index(stream) * 4 + hop
        return remote(sbuf.at[k], rbuf.at[k], rs_send.at[k], rs_recv.at[k], z_dev[stream[0]])

    def rs_start(stream):
        direction, sub = stream
        k = STREAMS.index(stream) * 4
        sbuf[k] = pacc[target(direction, REACH[stream]), pl.ds(sub * HALF, HALF), :].astype(BF16)
        rs_copy(stream, 0).start()

    def rs_step(stream, hop):
        direction, sub = stream
        k = STREAMS.index(stream) * 4 + hop
        rs_copy(stream, hop - 1).wait_recv()
        own = pacc[target(direction, REACH[stream] - hop), pl.ds(sub * HALF, HALF), :]
        sbuf[k] = (own + rbuf[k - 1].astype(F32)).astype(BF16)
        rs_copy(stream, hop).start()

    def relay(g):
        part_wait(part_copies(1, g, across_other))
        for copy in relay_copies(g):
            copy.start()

    def gather(g):
        part_wait(part_copies(0, g, across))
        merge(1 - s, g, *received(0, g), *received(1, g))
        part_wait(relay_copies(g))
        rows = pl.ds(g * HALF, HALF)
        merge(s, g, oacc[0, rows, :], mx[0, rows, 0:1], den[0, rows, 0:1], *received(2, g))

    relay(0)
    relay(1)
    gather(0)
    chunk(7, 0)
    rs_start(("R", 0))
    chunk(5, 0)
    rs_start(("L", 0))
    gather(1)
    chunk(7, 1)
    rs_start(("L", 1))
    chunk(6, 1)
    rs_start(("R", 1))
    for o, g in ((6, 0), (3, 0), (5, 1), (4, 1)):
        chunk(o, g)
    rs_step(("R", 0), 1)
    rs_step(("L", 0), 1)
    rs_step(("L", 1), 1)
    rs_step(("R", 1), 1)
    for o, g in ((4, 0), (1, 0), (3, 1), (2, 1)):
        chunk(o, g)
    rs_step(("R", 0), 2)
    rs_step(("L", 0), 2)
    rs_step(("L", 1), 2)
    rs_step(("R", 1), 2)
    for o, g in ((2, 0), (1, 1), (0, 0), (0, 1)):
        chunk(o, g)
    rs_step(("R", 0), 3)
    rs_step(("L", 1), 3)
    for sub in (0, 1):
        rows = pl.ds(sub * HALF, HALF)
        total = pacc[0, rows, :]
        for direction in ("R", "L"):
            stream = (direction, sub)
            k = STREAMS.index(stream) * 4 + REACH[stream] - 1
            rs_copy(stream, REACH[stream] - 1).wait_recv()
            total = total + rbuf[k].astype(F32)
        out[rows, :] = total.astype(BF16)

    for r in QUARTERS:
        for direction in ("R", "L"):
            for distance in range(1, REACH[direction, r % 2] + 1):
                z_copy(r, direction, distance).wait_send()
        for which in range(1, 8):
            kv_copy(kv.at[0, r], 0, r, which, partner).wait_send()

    @pl.when(s == 0)
    def _():
        for r in QUARTERS:
            x_copy(r).wait_send()
        for hh in (0, 1):
            wo_share(hh).wait_send()

    @pl.when(s == 1)
    def _():
        for r in QUARTERS:
            for copy in q_copies(r):
                copy.wait_send()
        for copy in wo_x_copies():
            copy.wait_send()

    for g in (0, 1):
        for copy in (*part_copies(0, g, across), *part_copies(1, g, across_other), *relay_copies(g)):
            copy.wait_send()
    for stream in STREAMS:
        for hop in range(REACH[stream]):
            rs_copy(stream, hop).wait_send()


def local(enc_states, dec_states, section_weights, group_lengths):
    dma = pltpu.SemaphoreType.DMA
    vmem = pltpu.VMEM
    return pl.pallas_call(
        kernel,
        out_shape=jax.ShapeDtypeStruct((ROWS, DH), BF16),
        in_specs=[pl.BlockSpec(memory_space=pl.ANY)] * 3 + [pl.BlockSpec(memory_space=pltpu.SMEM)],
        out_specs=pl.BlockSpec(memory_space=pltpu.VMEM),
        scratch_shapes=[
            vmem((NZ, ROWS, FEAT), BF16),
            vmem((2, FEAT, 2, FEAT), BF16),
            vmem((NZ, FEAT, FEAT), BF16),
            vmem((NZ, FEAT, FEAT), BF16),
            vmem((4, FEAT, FEAT), BF16),
            vmem((2, ROWS, FEAT), F32),
            vmem((8, 4, BLOCK, DH), BF16),
            vmem((4, BLOCK, DH), BF16),
            vmem((2, ROWS, DH), BF16),
            vmem((ROWS, DH), BF16),
            vmem((ROWS, FEAT), BF16),
            vmem((2, ROWS, DH), BF16),
            vmem((2, ROWS, DH), F32),
            vmem((2, ROWS, 128), F32),
            vmem((2, ROWS, 128), F32),
            vmem((2, ROWS, DH), BF16),
            vmem((2, 2, 16, HALF), F32),
            vmem((3, ROWS, DH), BF16),
            vmem((3, 2, 16, HALF), F32),
            vmem((NZ, ROWS, DH), F32),
            vmem((16, HALF, DH), BF16),
            vmem((16, HALF, DH), BF16),
            dma((3,)),
            dma((2,)),
            dma((32,)),
            dma((32,)),
            dma((32,)),
            dma((32,)),
            dma((12,)),
            dma((8,)),
            dma((4,)),
            dma((4,)),
            dma((12,)),
            dma((12,)),
            dma((16,)),
            dma((16,)),
        ],
        compiler_params=pltpu.CompilerParams(
            collective_id=0, has_side_effects=True, vmem_limit_bytes=60 * 2**20
        ),
    )(enc_states, dec_states, section_weights, group_lengths)


def solution(mesh):
    in_specs = (P("seq", "mp"), P("seq", "mp"), P("segment", None, None, "mp"), P("seq"))
    out_specs = P("seq", ("segment", "mp"))
    return jax.shard_map(local, mesh=mesh, in_specs=in_specs, out_specs=out_specs, check_vma=False)
```

time: 84.8 us -> 81.4 us (0.960)
  Pallas kernels: 83.1 us -> 79.2 us
    pallas_call x1, Pallas kernels: 83.1 us -> 79.2 us  [local(): pl.pallas_call(kernel, out_shape=jax.ShapeDtypeStruct((ROWS, DH), BF16),...]
where the time goes in v4:
time: 81.4 us; the launch traced here: 80.7 us
  Pallas kernels  79.2 us (97%)
  local copies, waits for them, and re-layouts  1.57 us (2%)
    pallas_call x1, Pallas kernels, local(): pl.pallas_call(kernel, out_shape=jax.ShapeDtypeStruct((ROWS, DH), BF16),...  79.2 us

profile of v4, /device:TPU:2, one launch (start us, length us, event | category | flops | bytes accessed | tf_op | source)
XLA Modules:
  0.0 80.7 jit_solution(2002753277086770764)
XLA Ops:
  0.0 79.2 %shard_map.46 = bf16[256,256]{1,0:T(8,128)(2,1)} custom-call(bf16[256,512]{1,0:T(8,128)(2,1)} %enc.1, bf16[256,512]{1,0:T(8,128)(2,1)} %dec.1, bf16[1,4096,2,512]{3,2,1,0:T(2,128)(2,1)} %weights.1, s32[2]{0:T(128)} %lengths.1), custom_call_target="tpu_custom_call" | custom-call | tf_op jit(solution)/shard_map/pallas_call | solution.py:534
  79.2 1.6 %copy.6 = bf16[256,256]{1,0:T(8,128)(2,1)} copy(bf16[256,256]{1,0:T(8,128)(2,1)} %shard_map.46) | data formatting | bytes 262144

commit v5 on v4

--- a/solution.py
+++ b/solution.py
@@ -16,7 +16,6 @@
 OFFSETS = (0, -1, 1, -2, 2, -3, 3, 4)
 REACH = {("R", 0): 4, ("R", 1): 3, ("L", 1): 4, ("L", 0): 3}
 QUARTERS = (0, 1, 2, 3)
-STREAMS = (("R", 0), ("L", 1), ("R", 1), ("L", 0))
 NT = (((1,), (1,)), ((), ()))
 
 
@@ -226,29 +225,31 @@
         oacc[k] = oacc[k] * shrink + jnp.dot(probs, values, preferred_element_type=F32)
 
     def part_copies(k, g, device):
-        rows = pl.ds(g * HALF, HALF)
-        sems = (k * 2 + g) * 2
-        return (
-            remote(ps.at[k, rows], pr.at[k, rows], p_send.at[sems], p_recv.at[sems], device),
-            remote(psm.at[k, g], prm.at[k, g], p_send.at[sems + 1], p_recv.at[sems + 1], device),
-        )
+        rows = pl.ds(g * QUART, QUART)
+        data = remote(ps.at[k, rows], pr.at[k, rows], p_send.at[k * 6 + g], p_recv.at[k * 6 + g], device)
+        if g % 2:
+            return (data,)
+        n = k * 6 + 4 + g // 2
+        return (remote(psm.at[k, g // 2], prm.at[k, g // 2], p_send.at[n], p_recv.at[n], device), data)
 
     def part_send(k):
-        for g in (0, 1):
-            rows = pl.ds(g * HALF, HALF)
+        for g in QUARTERS:
+            rows = pl.ds(g * QUART, QUART)
             ps[k, rows, :] = oacc[k, rows, :].astype(BF16)
-            psm[k, g, pl.ds(0, 8), :] = jnp.transpose(mx[k, rows, :])[0:8]
-            psm[k, g, pl.ds(8, 8), :] = jnp.transpose(den[k, rows, :])[0:8]
+            if g % 2 == 0:
+                both = pl.ds(g * QUART, HALF)
+                psm[k, g // 2, pl.ds(0, 8), :] = jnp.transpose(mx[k, both, :])[0:8]
+                psm[k, g // 2, pl.ds(8, 8), :] = jnp.transpose(den[k, both, :])[0:8]
             for copy in part_copies(k, g, across if k == 0 else across_other):
                 copy.start()
 
     def relay_copies(g):
-        rows = pl.ds(g * HALF, HALF)
-        sems = 8 + 2 * g
-        return (
-            remote(pr.at[1, rows], pr.at[2, rows], p_send.at[sems], p_recv.at[sems], across),
-            remote(prm.at[1, g], prm.at[2, g], p_send.at[sems + 1], p_recv.at[sems + 1], across),
-        )
+        rows = pl.ds(g * QUART, QUART)
+        data = remote(pr.at[1, rows], pr.at[2, rows], p_send.at[12 + g], p_recv.at[12 + g], across)
+        if g % 2:
+            return (data,)
+        n = 16 + g // 2
+        return (remote(prm.at[1, g // 2], prm.at[2, g // 2], p_send.at[n], p_recv.at[n], across), data)
 
     def column(row):
         return jnp.transpose(jnp.broadcast_to(row, (128, HALF)))[:, 0:1]
@@ -303,61 +304,63 @@
         def _():
             body(*args)
 
-    z_start(0, 1, 2)
+    z_start(0, 1)
     mx[...] = jnp.full_like(mx, NEG)
     den[...] = jnp.zeros_like(den)
     oacc[...] = jnp.zeros_like(oacc)
     split(0)
+    split(1)
     project(0, 2, 0)
     z_step(0, 1)
     z_step(1, 1)
-    z_start(3)
-    split(1)
+    z_start(2, 3)
+    split(2)
+    split(3)
     project(0, 2, 1)
-    split(2)
     project(0, 2, 2)
-    z_step(2, 1)
     z_step(0, 2)
     z_step(1, 2)
-    split(3)
+    split(4)
+    split(5)
     project(0, 2, 3)
-    split(4)
     project(0, 2, 4)
+    z_step(2, 1)
     z_step(3, 1)
-    z_step(2, 2)
+    split(6)
+    split(7)
+
+    @pl.when(s == 1)
+    def _():
+        for copy in wo_x_copies():
+            copy.start()
+        wo_local().start()
+
     z_step(0, 3)
     z_step(1, 3)
-    split(5)
+    z_step(2, 2)
+    z_step(3, 2)
     project(0, 2, 5)
-    split(6)
     project(0, 2, 6)
-    split(7)
-    z_step(2, 3)
-    z_step(3, 2)
     z_step(0, 4)
     z_step(1, 4)
     project(0, 2, 7)
     finish(0)
     finish(1)
-
-    @pl.when(s == 1)
-    def _():
-        for copy in wo_x_copies():
-            copy.start()
-        wo_local().start()
-
-    for o in range(7):
-        project(2, 3, o)
-    z_step(2, 4)
+    project(2, 4, 0)
+    project(2, 4, 1)
+    project(2, 4, 2)
+    project(2, 4, 3)
+    z_step(2, 3)
     z_step(3, 3)
-    project(2, 3, 7)
-    finish(2)
-    for o in range(7):
-        project(3, 4, o)
+    project(2, 4, 4)
+    project(2, 4, 5)
+    project(2, 4, 6)
     dec_side(y_near, 0, False)
     dec_side(y_near, 1, False)
+    z_step(2, 4)
     z_step(3, 4)
-    project(3, 4, 7)
+    project(2, 4, 7)
+    finish(2)
     finish(3)
     y_next(0)
     dec_side(y_near, 2, False)
@@ -430,23 +433,25 @@
             return 7
         return 2 * distance - (0 if direction == "R" else 1)
 
-    def rs_copy(stream, hop):
-        k = STREAMS.index(stream) * 4 + hop
-        return remote(sbuf.at[k], rbuf.at[k], rs_send.at[k], rs_recv.at[k], z_dev[stream[0]])
-
-    def rs_start(stream):
-        direction, sub = stream
-        k = STREAMS.index(stream) * 4
-        sbuf[k] = pacc[target(direction, REACH[stream]), pl.ds(sub * HALF, HALF), :].astype(BF16)
-        rs_copy(stream, 0).start()
-
-    def rs_step(stream, hop):
-        direction, sub = stream
-        k = STREAMS.index(stream) * 4 + hop
-        rs_copy(stream, hop - 1).wait_recv()
-        own = pacc[target(direction, REACH[stream] - hop), pl.ds(sub * HALF, HALF), :]
-        sbuf[k] = (own + rbuf[k - 1].astype(F32)).astype(BF16)
-        rs_copy(stream, hop).start()
+    def rs_copy(direction, r, hop):
+        k = (r * 2 + (direction == "L")) * 4 + hop
+        return remote(sbuf.at[k], rbuf.at[k], rs_send.at[k], rs_recv.at[k], z_dev[direction])
+
+    def rs_start(direction, r):
+        k = (r * 2 + (direction == "L")) * 4
+        sbuf[k] = pacc[target(direction, REACH[direction, r % 2]), pl.ds(r * QUART, QUART), :].astype(BF16)
+        rs_copy(direction, r, 0).start()
+
+    def rs_step(hop, *quarters):
+        for r in quarters:
+            for direction in ("R", "L") if r % 2 == 0 else ("L", "R"):
+                reach = REACH[direction, r % 2]
+                if hop < reach:
+                    k = (r * 2 + (direction == "L")) * 4 + hop
+                    rs_copy(direction, r, hop - 1).wait_recv()
+                    own = pacc[target(direction, reach - hop), pl.ds(r * QUART, QUART), :]
+                    sbuf[k] = (own + rbuf[k - 1].astype(F32)).astype(BF16)
+                    rs_copy(direction, r, hop).start()
 
     def relay(g):
         part_wait(part_copies(1, g, across_other))
@@ -454,48 +459,48 @@
             copy.start()
 
     def gather(g):
-        part_wait(part_copies(0, g, across))
+        for r in (2 * g, 2 * g + 1):
+            part_wait(part_copies(0, r, across))
         merge(1 - s, g, *received(0, g), *received(1, g))
-        part_wait(relay_copies(g))
+        for r in (2 * g, 2 * g + 1):
+            part_wait(relay_copies(r))
         rows = pl.ds(g * HALF, HALF)
         merge(s, g, oacc[0, rows, :], mx[0, rows, 0:1], den[0, rows, 0:1], *received(2, g))
 
-    relay(0)
-    relay(1)
-    gather(0)
-    chunk(7, 0)
-    rs_start(("R", 0))
-    chunk(5, 0)
-    rs_start(("L", 0))
-    gather(1)
-    chunk(7, 1)
-    rs_start(("L", 1))
-    chunk(6, 1)
-    rs_start(("R", 1))
-    for o, g in ((6, 0), (3, 0), (5, 1), (4, 1)):
-        chunk(o, g)
-    rs_step(("R", 0), 1)
-    rs_step(("L", 0), 1)
-    rs_step(("L", 1), 1)
-    rs_step(("R", 1), 1)
-    for o, g in ((4, 0), (1, 0), (3, 1), (2, 1)):
-        chunk(o, g)
-    rs_step(("R", 0), 2)
-    rs_step(("L", 0), 2)
-    rs_step(("L", 1), 2)
-    rs_step(("R", 1), 2)
-    for o, g in ((2, 0), (1, 1), (0, 0), (0, 1)):
-        chunk(o, g)
-    rs_step(("R", 0), 3)
-    rs_step(("L", 1), 3)
-    for sub in (0, 1):
-        rows = pl.ds(sub * HALF, HALF)
+    for g in QUARTERS:
+        relay(g)
+    for g in (0, 1):
+        gather(g)
+        chunk(7, g)
+        rs_start("R", 2 * g)
+        rs_start("L", 2 * g + 1)
+        chunk(5, g)
+        rs_start("L", 2 * g)
+        chunk(6, g)
+        rs_start("R", 2 * g + 1)
+    chunk(3, 0)
+    chunk(4, 0)
+    rs_step(1, 0, 1)
+    chunk(3, 1)
+    chunk(4, 1)
+    rs_step(1, 2, 3)
+    chunk(1, 0)
+    chunk(2, 0)
+    rs_step(2, 0, 1)
+    chunk(1, 1)
+    chunk(2, 1)
+    rs_step(2, 2, 3)
+    chunk(0, 0)
+    rs_step(3, 0, 1)
+    chunk(0, 1)
+    rs_step(3, 2, 3)
+    for r in QUARTERS:
+        rows = pl.ds(r * QUART, QUART)
         total = pacc[0, rows, :]
-        for direction in ("R", "L"):
-            stream = (direction, sub)
-            k = STREAMS.index(stream) * 4 + REACH[stream] - 1
-            rs_copy(stream, REACH[stream] - 1).wait_recv()
-            total = total + rbuf[k].astype(F32)
+        for direction in ("R", "L") if r % 2 else ("L", "R"):
+            hop = REACH[direction, r % 2] - 1
+            rs_copy(direction, r, hop).wait_recv()
+            total = total + rbuf[(r * 2 + (direction == "L")) * 4 + hop].astype(F32)
         out[rows, :] = total.astype(BF16)
 
     for r in QUARTERS:
@@ -520,12 +525,12 @@
         for copy in wo_x_copies():
             copy.wait_send()
 
-    for g in (0, 1):
-        for copy in (*part_copies(0, g, across), *part_copies(1, g, across_other), *relay_copies(g)):
+    for r in QUARTERS:
+        for copy in (*part_copies(0, r, across), *part_copies(1, r, across_other), *relay_copies(r)):
             copy.wait_send()
-    for stream in STREAMS:
-        for hop in range(REACH[stream]):
-            rs_copy(stream, hop).wait_send()
+        for direction in ("R", "L"):
+            for hop in range(REACH[direction, r % 2]):
+                rs_copy(direction, r, hop).wait_send()
 
 
 def local(enc_states, dec_states, section_weights, group_lengths):
@@ -557,8 +562,8 @@
             vmem((3, ROWS, DH), BF16),
             vmem((3, 2, 16, HALF), F32),
             vmem((NZ, ROWS, DH), F32),
-            vmem((16, HALF, DH), BF16),
-            vmem((16, HALF, DH), BF16),
+            vmem((32, QUART, DH), BF16),
+            vmem((32, QUART, DH), BF16),
             dma((3,)),
             dma((2,)),
             dma((32,)),
@@ -569,10 +574,10 @@
             dma((8,)),
             dma((4,)),
             dma((4,)),
-            dma((12,)),
-            dma((12,)),
-            dma((16,)),
-            dma((16,)),
+            dma((18,)),
+            dma((18,)),
+            dma((32,)),
+            dma((32,)),
         ],
         compiler_params=pltpu.CompilerParams(
             collective_id=0, has_side_effects=True, vmem_limit_bytes=60 * 2**20

time: 81.4 us -> 78.3 us (0.962)
  Pallas kernels: 79.2 us -> 75.5 us
    pallas_call x1, Pallas kernels: 79.2 us -> 75.5 us  [local(): pl.pallas_call(kernel, out_shape=jax.ShapeDtypeStruct((ROWS, DH), BF16),...]
where the time goes in v5:
time: 78.3 us; the launch traced here: 77.1 us
  Pallas kernels  75.5 us (96%)
  local copies, waits for them, and re-layouts  1.57 us (2%)
    pallas_call x1, Pallas kernels, local(): pl.pallas_call(kernel, out_shape=jax.ShapeDtypeStruct((ROWS, DH), BF16),...  75.5 us
    unnamed x1, local copies, waits for them, and re-layouts  1.57 us

profile of v5, /device:TPU:2, one launch (start us, length us, event | category | flops | bytes accessed | tf_op | source)
XLA Modules:
  0.0 77.1 jit_solution(5022814724672109676)
XLA Ops:
  0.0 75.5 %shard_map.46 = bf16[256,256]{1,0:T(8,128)(2,1)} custom-call(bf16[256,512]{1,0:T(8,128)(2,1)} %enc.1, bf16[256,512]{1,0:T(8,128)(2,1)} %dec.1, bf16[1,4096,2,512]{3,2,1,0:T(2,128)(2,1)} %weights.1, s32[2]{0:T(128)} %lengths.1), custom_call_target="tpu_custom_call" | custom-call | tf_op jit(solution)/shard_map/pallas_call | solution.py:539
  75.5 1.6 %copy.6 = bf16[256,256]{1,0:T(8,128)(2,1)} copy(bf16[256,256]{1,0:T(8,128)(2,1)} %shard_map.46) | data formatting | bytes 262144

commit v6 on v5

--- a/solution.py
+++ b/solution.py
@@ -28,7 +28,7 @@
 
 
 def kernel(enc, dec, weights, lengths, out, xg, stage, w0, w1, wo, acc, kv, ks, qbuf, qs, dres, att, oacc,
-           mx, den, ps, psm, pr, prm, pacc, sbuf, rbuf, load_sem, stage_sem, z_send, z_recv, kv_send, kv_recv, q_send, q_recv,
+           mx, den, pacc, sbuf, rbuf, load_sem, stage_sem, z_send, z_recv, kv_send, kv_recv, q_send, q_recv,
            wo_send, wo_recv, p_send, p_recv, rs_send, rs_recv):
     s = lax.axis_index("segment")
     q = lax.axis_index("seq")
@@ -138,29 +138,28 @@
             else:
                 acc[1, rows, :] += second
 
-    def kv_copy(src, index, r, which, device):
-        return remote(src, kv.at[index, r], kv_send.at[r * 8 + which], kv_recv.at[r * 8 + index], device)
-
-    def kv_wait(index, r):
-        kv_copy(kv.at[index, r], index, r, 0, partner).wait_recv()
-
-    def forward(index, r, which, device):
-        kv_copy(kv.at[index, r], index, r, which, device).start()
-
-    def x_copy(r):
-        return kv_copy(ks.at[r], y * 2 + c, r, 0, across)
-
-    def q_copies(r):
+    def kv_copy(src, source, r, which, device):
+        return remote(src, kv.at[source, r], kv_send.at[r * 17 + which], kv_recv.at[r * 16 + source], device)
+
+    def kv_wait(source, r):
+        kv_copy(kv.at[source, r], source, r, 0, partner).wait_recv()
+
+    def forward(source, r, which, device):
+        kv_copy(kv.at[source, r], source, r, which, device).start()
+
+    def x_copies(r):
+        return (
+            kv_copy(ks.at[r], q, r, 0, across_other),
+            kv_copy(kv.at[q, r], q, r, 1, same_other),
+            kv_copy(ks.at[r], q, r, 2, across),
+        )
+
+    def q_copy(r):
         rows = pl.ds(r * QUART, QUART)
-        return (
-            remote(qs.at[rows], qbuf.at[0, rows], q_send.at[r * 3], q_recv.at[r * 2], across),
-            remote(qs.at[rows], qbuf.at[1, rows], q_send.at[r * 3 + 1], q_recv.at[r * 2 + 1], across_other),
-            remote(qbuf.at[0, rows], qbuf.at[1, rows], q_send.at[r * 3 + 2], q_recv.at[r * 2 + 1], same_other),
-        )
+        return remote(qs.at[rows], qbuf.at[rows], q_send.at[r], q_recv.at[r], across)
 
     def finish(r):
         rows = pl.ds(r * QUART, QUART)
-        own = y * 2 + c
 
         @pl.when(s == 0)
         def _():
@@ -170,103 +169,70 @@
             ks[r, pl.ds(0, QUART), :] = acc[0, rows, DH:].astype(BF16)
             ks[r, pl.ds(QUART, QUART), :] = acc[1, rows, DH:].astype(BF16)
             ks[r, pl.ds(2 * QUART, 16), :] = bias
-            x_copy(r).start()
-            kv[own, r, pl.ds(0, QUART), :] = acc[0, rows, :DH].astype(BF16)
-            kv[own, r, pl.ds(QUART, QUART), :] = acc[1, rows, :DH].astype(BF16)
-            kv[own, r, pl.ds(2 * QUART, 16), :] = bias
-            y_near(r, True)
+            kv[q, r, pl.ds(0, QUART), :] = acc[0, rows, :DH].astype(BF16)
+            kv[q, r, pl.ds(QUART, QUART), :] = acc[1, rows, :DH].astype(BF16)
+            kv[q, r, pl.ds(2 * QUART, 16), :] = bias
+            for copy in x_copies(r):
+                copy.start()
+            y_near(r, 0, True)
 
         @pl.when(s == 1)
         def _():
             scale = DH ** -0.5
             qs[rows, :] = acc[0, rows, :DH].astype(BF16) * jnp.asarray(scale, BF16)
-            qbuf[0, rows, :] = acc[0, rows, DH:].astype(BF16) * jnp.asarray(scale, BF16)
-            for copy in q_copies(r):
-                copy.start()
-
-    def y_near(r, local_source):
-        index = y * 2 + c
+            qbuf[rows, :] = acc[0, rows, DH:].astype(BF16) * jnp.asarray(scale, BF16)
+            q_copy(r).start()
+
+    def source_of(yy, k):
+        return seq_of(yy, xh if k == 0 else 1 - xh, c)
+
+    def y_near(r, k, local_source):
+        source = source_of(y, k)
         if not local_source:
-            kv_wait(index, r)
-        forward(index, r, 1, up)
-        forward(index, r, 2, down)
-        forward(index, r, 3, partner)
-
-    def y_next(r):
-        low, high = y_down * 2 + c, y_up * 2 + c
-        one, other = ((low, up, 5, 6), high) if r % 2 == 0 else ((high, down, 6, 5), low)
-        index, device, share_one, share_other = one
-        kv_wait(index, r)
-        forward(index, r, 4, device)
-        forward(index, r, share_one, partner)
+            kv_wait(source, r)
+        forward(source, r, 3 + 2 * k, up)
+        forward(source, r, 4 + 2 * k, down)
+        forward(source, r, 8 + k, partner)
+
+    def y_next(r, k):
+        low, high = source_of(y_down, k), source_of(y_up, k)
+        one, device, share, other, other_share = (
+            (low, up, 11 + k, high, 13 + k) if (r + k) % 2 == 0 else (high, down, 13 + k, low, 11 + k)
+        )
+        kv_wait(one, r)
+        forward(one, r, 7 if k == 0 else 10, device)
+        forward(one, r, share, partner)
         kv_wait(other, r)
-        forward(other, r, share_other, partner)
-
-    def y_last(r):
-        kv_wait(y_far * 2 + c, r)
-        forward(y_far * 2 + c, r, 7, partner)
+        forward(other, r, other_share, partner)
+
+    def y_last(r, k):
+        kv_wait(source_of(y_far, k), r)
+        forward(source_of(y_far, k), r, 15 + k, partner)
 
     def shared_wait(r):
         for yy in (y, y_down, y_up, y_far):
-            kv_wait(yy * 2 + 1 - c, r)
-
-    def attend(r, k):
-        keys = jnp.concatenate([kv[b, r, pl.ds(0, QUART), :] for b in range(8)], axis=0)
-        values = jnp.concatenate([kv[b, r, pl.ds(QUART, QUART), :] for b in range(8)], axis=0)
-        signs = [kv[b, r, pl.ds(2 * QUART, 16), pl.ds(0, GROUP)].astype(F32)[0:1] for b in range(8)]
-        bias = jnp.concatenate([signs[b] + signs[b + 1] for b in range(0, 8, 2)], axis=1)
-        best, total = mx[k, :, 0:1], den[k, :, 0:1]
-        scores = lax.dot_general(qbuf[k], keys, NT, preferred_element_type=F32) + bias
-        new_best = jnp.maximum(best, jnp.max(scores, axis=1, keepdims=True))
-        shrink = jnp.exp(best - new_best)
-        probs = jnp.exp(scores - new_best).astype(BF16)
-        mx[k] = jnp.broadcast_to(new_best, (ROWS, 128))
-        den[k] = jnp.broadcast_to(total * shrink + jnp.sum(probs.astype(F32), axis=1, keepdims=True), (ROWS, 128))
-        oacc[k] = oacc[k] * shrink + jnp.dot(probs, values, preferred_element_type=F32)
-
-    def part_copies(k, g, device):
-        rows = pl.ds(g * QUART, QUART)
-        data = remote(ps.at[k, rows], pr.at[k, rows], p_send.at[k * 6 + g], p_recv.at[k * 6 + g], device)
-        if g % 2:
-            return (data,)
-        n = k * 6 + 4 + g // 2
-        return (remote(psm.at[k, g // 2], prm.at[k, g // 2], p_send.at[n], p_recv.at[n], device), data)
-
-    def part_send(k):
-        for g in QUARTERS:
-            rows = pl.ds(g * QUART, QUART)
-            ps[k, rows, :] = oacc[k, rows, :].astype(BF16)
-            if g % 2 == 0:
-                both = pl.ds(g * QUART, HALF)
-                psm[k, g // 2, pl.ds(0, 8), :] = jnp.transpose(mx[k, both, :])[0:8]
-                psm[k, g // 2, pl.ds(8, 8), :] = jnp.transpose(den[k, both, :])[0:8]
-            for copy in part_copies(k, g, across if k == 0 else across_other):
-                copy.start()
-
-    def relay_copies(g):
-        rows = pl.ds(g * QUART, QUART)
-        data = remote(pr.at[1, rows], pr.at[2, rows], p_send.at[12 + g], p_recv.at[12 + g], across)
-        if g % 2:
-            return (data,)
-        n = 16 + g // 2
-        return (remote(prm.at[1, g // 2], prm.at[2, g // 2], p_send.at[n], p_recv.at[n], across), data)
-
-    def column(row):
-        return jnp.transpose(jnp.broadcast_to(row, (128, HALF)))[:, 0:1]
-
-    def merge(head, g, one, one_best, one_sum, two, two_best, two_sum):
-        best = jnp.maximum(one_best, two_best)
-        one_share, two_share = jnp.exp(one_best - best), jnp.exp(two_best - best)
-        scale = 1.0 / (one_sum * one_share + two_sum * two_share)
-        att[head, pl.ds(g * HALF, HALF), :] = (one * (one_share * scale) + two * (two_share * scale)).astype(BF16)
-
-    def received(slot, g):
-        rows = pl.ds(g * HALF, HALF)
-        return pr[slot, rows, :].astype(F32), column(prm[slot, g, 0:1, :]), column(prm[slot, g, 8:9, :])
-
-    def part_wait(copies):
-        for copy in copies:
-            copy.wait_recv()
+            for hh in (0, 1):
+                kv_wait(seq_of(yy, hh, 1 - c), r)
+
+    def attend(r):
+        for first in (0, 8):
+            blocks = range(first, first + 8)
+            keys = jnp.concatenate([kv[b, r, pl.ds(0, QUART), :] for b in blocks], axis=0)
+            values = jnp.concatenate([kv[b, r, pl.ds(QUART, QUART), :] for b in blocks], axis=0)
+            signs = [kv[b, r, pl.ds(2 * QUART, 16), pl.ds(0, GROUP)].astype(F32)[0:1] for b in blocks]
+            bias = jnp.concatenate([signs[b] + signs[b + 1] for b in range(0, 8, 2)], axis=1)
+            best, total = mx[:, 0:1], den[:, 0:1]
+            scores = lax.dot_general(qbuf[...], keys, NT, preferred_element_type=F32) + bias
+            new_best = jnp.maximum(best, jnp.max(scores, axis=1, keepdims=True))
+            shrink = jnp.exp(best - new_best)
+            probs = jnp.exp(scores - new_best).astype(BF16)
+            mx[:, 0:1] = new_best
+            den[:, 0:1] = total * shrink + jnp.sum(probs.astype(F32), axis=1, keepdims=True)
+            oacc[...] = oacc[...] * shrink + jnp.dot(probs, values, preferred_element_type=F32)
+
+    def att_copy(head, r):
+        rows = pl.ds(r * QUART, QUART)
+        return remote(att.at[head, rows], att.at[head, rows], p_send.at[r], p_recv.at[r], across)
 
     part = xh * 2 + c
 
@@ -355,40 +321,48 @@
     project(2, 4, 4)
     project(2, 4, 5)
     project(2, 4, 6)
-    dec_side(y_near, 0, False)
-    dec_side(y_near, 1, False)
+    dec_side(y_near, 0, 0, False)
+    dec_side(y_near, 0, 1, False)
     z_step(2, 4)
     z_step(3, 4)
     project(2, 4, 7)
     finish(2)
     finish(3)
-    y_next(0)
-    dec_side(y_near, 2, False)
-    y_next(1)
-    dec_side(y_near, 3, False)
-    y_next(2)
-    y_last(0)
-    y_last(1)
-    for r in QUARTERS:
-        q_copies(r)[1].wait_recv()
+    for k in (0, 1):
+        dec_side(y_near, 1, k, False)
+    y_next(0, 0)
+    enc_side(y_near, 0, 1, False)
+    y_next(1, 0)
+    enc_side(y_near, 1, 1, False)
+    y_next(0, 1)
+    for k in (0, 1):
+        dec_side(y_near, 2, k, False)
+    y_next(1, 1)
+    y_last(0, 0)
+    y_last(1, 0)
+    enc_side(y_near, 2, 1, False)
+    y_next(2, 0)
+    y_last(0, 1)
+    for k in (0, 1):
+        dec_side(y_near, 3, k, False)
+    enc_side(y_near, 3, 1, False)
+    y_last(1, 1)
 
     @pl.when(s == 0)
     def _():
         for r in QUARTERS:
-            q_copies(r)[0].wait_recv()
+            q_copy(r).wait_recv()
 
     shared_wait(0)
-    attend(0, 1)
-    attend(0, 0)
-    y_next(3)
+    attend(0)
+    y_next(2, 1)
+    y_next(3, 0)
     shared_wait(1)
-    attend(1, 1)
-    y_last(2)
-    attend(1, 0)
-    y_last(3)
-    shared_wait(2)
-    attend(2, 1)
-    attend(2, 0)
+    attend(1)
+    y_next(3, 1)
+    y_last(2, 0)
+    y_last(3, 0)
+    y_last(2, 1)
 
     @pl.when(s == 0)
     def _():
@@ -396,11 +370,15 @@
             wo_wait(hh * 2 + c)
             wo_share(hh).start()
 
+    shared_wait(2)
+    attend(2)
+    y_last(3, 1)
     shared_wait(3)
-    attend(3, 1)
-    part_send(1)
-    attend(3, 0)
-    part_send(0)
+    attend(3)
+    for r in QUARTERS:
+        rows = pl.ds(r * QUART, QUART)
+        att[s, rows, :] = (oacc[rows, :] / den[rows, 0:1]).astype(BF16)
+        att_copy(s, r).start()
 
     @pl.when(s == 0)
     def _():
@@ -453,24 +431,9 @@
                     sbuf[k] = (own + rbuf[k - 1].astype(F32)).astype(BF16)
                     rs_copy(direction, r, hop).start()
 
-    def relay(g):
-        part_wait(part_copies(1, g, across_other))
-        for copy in relay_copies(g):
-            copy.start()
-
-    def gather(g):
+    for g in (0, 1):
         for r in (2 * g, 2 * g + 1):
-            part_wait(part_copies(0, r, across))
-        merge(1 - s, g, *received(0, g), *received(1, g))
-        for r in (2 * g, 2 * g + 1):
-            part_wait(relay_copies(r))
-        rows = pl.ds(g * HALF, HALF)
-        merge(s, g, oacc[0, rows, :], mx[0, rows, 0:1], den[0, rows, 0:1], *received(2, g))
-
-    for g in QUARTERS:
-        relay(g)
-    for g in (0, 1):
-        gather(g)
+            att_copy(1 - s, r).wait_recv()
         chunk(7, g)
         rs_start("R", 2 * g)
         rs_start("L", 2 * g + 1)
@@ -507,27 +470,26 @@
         for direction in ("R", "L"):
             for distance in range(1, REACH[direction, r % 2] + 1):
                 z_copy(r, direction, distance).wait_send()
-        for which in range(1, 8):
+        for which in range(3, 17):
             kv_copy(kv.at[0, r], 0, r, which, partner).wait_send()
 
     @pl.when(s == 0)
     def _():
         for r in QUARTERS:
-            x_copy(r).wait_send()
+            for copy in x_copies(r):
+                copy.wait_send()
         for hh in (0, 1):
             wo_share(hh).wait_send()
 
     @pl.when(s == 1)
     def _():
         for r in QUARTERS:
-            for copy in q_copies(r):
-                copy.wait_send()
+            q_copy(r).wait_send()
         for copy in wo_x_copies():
             copy.wait_send()
 
     for r in QUARTERS:
-        for copy in (*part_copies(0, r, across), *part_copies(1, r, across_other), *relay_copies(r)):
-            copy.wait_send()
+        att_copy(s, r).wait_send()
         for direction in ("R", "L"):
             for hop in range(REACH[direction, r % 2]):
                 rs_copy(direction, r, hop).wait_send()
@@ -548,19 +510,15 @@
             vmem((NZ, FEAT, FEAT), BF16),
             vmem((4, FEAT, FEAT), BF16),
             vmem((2, ROWS, FEAT), F32),
-            vmem((8, 4, BLOCK, DH), BF16),
+            vmem((16, 4, BLOCK, DH), BF16),
             vmem((4, BLOCK, DH), BF16),
-            vmem((2, ROWS, DH), BF16),
+            vmem((ROWS, DH), BF16),
             vmem((ROWS, DH), BF16),
             vmem((ROWS, FEAT), BF16),
             vmem((2, ROWS, DH), BF16),
-            vmem((2, ROWS, DH), F32),
-            vmem((2, ROWS, 128), F32),
-            vmem((2, ROWS, 128), F32),
-            vmem((2, ROWS, DH), BF16),
-            vmem((2, 2, 16, HALF), F32),
-            vmem((3, ROWS, DH), BF16),
-            vmem((3, 2, 16, HALF), F32),
+            vmem((ROWS, DH), F32),
+            vmem((ROWS, 128), F32),
+            vmem((ROWS, 128), F32),
             vmem((NZ, ROWS, DH), F32),
             vmem((32, QUART, DH), BF16),
             vmem((32, QUART, DH), BF16),
@@ -568,14 +526,14 @@
             dma((2,)),
             dma((32,)),
             dma((32,)),
-            dma((32,)),
-            dma((32,)),
-            dma((12,)),
-            dma((8,)),
+            dma((68,)),
+            dma((64,)),
             dma((4,)),
             dma((4,)),
-            dma((18,)),
-            dma((18,)),
+            dma((4,)),
+            dma((4,)),
+            dma((4,)),
+            dma((4,)),
             dma((32,)),
             dma((32,)),
         ],

time: 78.3 us -> 81.8 us (1.045); the launches traced: 77.1 us -> 81.5 us
  Pallas kernels: 75.5 us -> 80 us
    pallas_call x1, Pallas kernels: 75.5 us -> 80 us  [local(): pl.pallas_call(kernel, out_shape=jax.ShapeDtypeStruct((ROWS, DH), BF16),...]
where the time goes in v6:
time: 81.8 us; the launch traced here: 81.5 us
  Pallas kernels  80 us (98%)
  local copies, waits for them, and re-layouts  1.57 us (2%)
    pallas_call x1, Pallas kernels, local(): pl.pallas_call(kernel, out_shape=jax.ShapeDtypeStruct((ROWS, DH), BF16),...  80 us

profile of v6, /device:TPU:2, one launch (start us, length us, event | category | flops | bytes accessed | tf_op | source)
XLA Modules:
  0.0 81.5 jit_solution(5808776482263628604)
XLA Ops:
  0.0 80.0 %shard_map.46 = bf16[256,256]{1,0:T(8,128)(2,1)} custom-call(bf16[256,512]{1,0:T(8,128)(2,1)} %enc.1, bf16[256,512]{1,0:T(8,128)(2,1)} %dec.1, bf16[1,4096,2,512]{3,2,1,0:T(2,128)(2,1)} %weights.1, s32[2]{0:T(128)} %lengths.1), custom_call_target="tpu_custom_call" | custom-call | tf_op jit(solution)/shard_map/pallas_call | solution.py:501
  80.0 1.6 %copy.6 = bf16[256,256]{1,0:T(8,128)(2,1)} copy(bf16[256,256]{1,0:T(8,128)(2,1)} %shard_map.46) | data formatting | bytes 262144

commit v7 on v5

--- a/solution.py
+++ b/solution.py
@@ -16,6 +16,7 @@
 OFFSETS = (0, -1, 1, -2, 2, -3, 3, 4)
 REACH = {("R", 0): 4, ("R", 1): 3, ("L", 1): 4, ("L", 0): 3}
 QUARTERS = (0, 1, 2, 3)
+DIRECT = (2, 3)
 NT = (((1,), (1,)), ((), ()))
 
 
@@ -42,6 +43,7 @@
     y_up, y_down, y_far = (y + 1) % 4, (y + 3) % 4, (y + 2) % 4
     partner = (s, seq_of(y, xh, 1 - c), m)
     up, down = (s, seq_of(y_up, xh, c), m), (s, seq_of(y_down, xh, c), m)
+    far = (s, seq_of(y_far, xh, c), m)
     across = (1 - s, q, m)
     across_other = (1 - s, seq_of(y, 1 - xh, c), m)
     same_other = (s, seq_of(y, 1 - xh, c), m)
@@ -77,7 +79,7 @@
     stage_copy(1).start()
 
     barrier = pltpu.get_barrier_semaphore()
-    peers = (z_dev["R"], z_dev["L"], up, down, partner, across, across_other, same_other)
+    peers = (z_dev["R"], z_dev["L"], up, down, far, partner, across, across_other, same_other)
     for peer in peers:
         pl.semaphore_signal(barrier, inc=1, device_id=peer, device_id_type=MESH)
     pl.semaphore_wait(barrier, len(peers))
@@ -188,6 +190,8 @@
         index = y * 2 + c
         if not local_source:
             kv_wait(index, r)
+        if r in DIRECT:
+            forward(index, r, 4, far)
         forward(index, r, 1, up)
         forward(index, r, 2, down)
         forward(index, r, 3, partner)
@@ -197,7 +201,8 @@
         one, other = ((low, up, 5, 6), high) if r % 2 == 0 else ((high, down, 6, 5), low)
         index, device, share_one, share_other = one
         kv_wait(index, r)
-        forward(index, r, 4, device)
+        if r not in DIRECT:
+            forward(index, r, 4, device)
         forward(index, r, share_one, partner)
         kv_wait(other, r)
         forward(other, r, share_other, partner)

time: 78.3 us -> 77 us (0.983); the launches traced: 77.1 us -> 76.7 us
  no operation moved by 1% of the time
where the time goes in v7:
time: 77 us; the launch traced here: 76.7 us
  Pallas kernels  75.1 us (98%)
  local copies, waits for them, and re-layouts  1.57 us (2%)
    pallas_call x1, Pallas kernels, local(): pl.pallas_call(kernel, out_shape=jax.ShapeDtypeStruct((ROWS, DH), BF16),...  75.1 us
    unnamed x1, local copies, waits for them, and re-layouts  1.57 us

profile of v7, /device:TPU:2, one launch (start us, length us, event | category | flops | bytes accessed | tf_op | source)
XLA Modules:
  0.0 76.7 jit_solution(13903576636395561653)
XLA Ops:
  0.0 75.1 %shard_map.46 = bf16[256,256]{1,0:T(8,128)(2,1)} custom-call(bf16[256,512]{1,0:T(8,128)(2,1)} %enc.1, bf16[256,512]{1,0:T(8,128)(2,1)} %dec.1, bf16[1,4096,2,512]{3,2,1,0:T(2,128)(2,1)} %weights.1, s32[2]{0:T(128)} %lengths.1), custom_call_target="tpu_custom_call" | custom-call | tf_op jit(solution)/shard_map/pallas_call | solution.py:544
  75.1 1.6 %copy.6 = bf16[256,256]{1,0:T(8,128)(2,1)} copy(bf16[256,256]{1,0:T(8,128)(2,1)} %shard_map.46) | data formatting | bytes 262144

commit v8 on v7

--- a/solution.py
+++ b/solution.py
@@ -393,7 +393,6 @@
     y_last(3)
     shared_wait(2)
     attend(2, 1)
-    attend(2, 0)
 
     @pl.when(s == 0)
     def _():
@@ -404,6 +403,7 @@
     shared_wait(3)
     attend(3, 1)
     part_send(1)
+    attend(2, 0)
     attend(3, 0)
     part_send(0)
 

time: 77 us -> 77 us (level)
  no operation moved by 1% of the time
where the time goes in v8:
time: 77 us; the launch traced here: 76.4 us
  Pallas kernels  74.8 us (97%)
  local copies, waits for them, and re-layouts  1.57 us (2%)
    pallas_call x1, Pallas kernels, local(): pl.pallas_call(kernel, out_shape=jax.ShapeDtypeStruct((ROWS, DH), BF16),...  74.8 us
    unnamed x1, local copies, waits for them, and re-layouts  1.57 us

profile of v8, /device:TPU:2, one launch (start us, length us, event | category | flops | bytes accessed | tf_op | source)
XLA Modules:
  0.0 76.4 jit_solution(1322845595371247525)
XLA Ops:
  0.0 74.8 %shard_map.46 = bf16[256,256]{1,0:T(8,128)(2,1)} custom-call(bf16[256,512]{1,0:T(8,128)(2,1)} %enc.1, bf16[256,512]{1,0:T(8,128)(2,1)} %dec.1, bf16[1,4096,2,512]{3,2,1,0:T(2,128)(2,1)} %weights.1, s32[2]{0:T(128)} %lengths.1), custom_call_target="tpu_custom_call" | custom-call | tf_op jit(solution)/shard_map/pallas_call | solution.py:544
  74.9 1.6 %copy.6 = bf16[256,256]{1,0:T(8,128)(2,1)} copy(bf16[256,256]{1,0:T(8,128)(2,1)} %shard_map.46) | data formatting | bytes 262144
